TPU v7x, 32 devices: a whole 2x2x4 slice. The times are simulated.
32 devices in a mesh: fsdp: 16 (over z, y, x), tp: 2 (over core).
Axes of the slice: x: 2, y: 2, z: 4, core: 2. Of those that a mesh axis runs over, the one named last changes fastest.
Arguments:
- tokens: bfloat16 [2, 2048, 8192], P(None, 'fsdp', 'tp'), may hold values from -6 to 6
- frozen_weight: bfloat16 [8192, 2048], P('tp', 'fsdp'), may hold values from -0.0625 to 0.0625
- cotangent: bfloat16 [2, 2048, 2048], P(None, 'fsdp'), may hold values from -6 to 6
- block_adapter_index: int32 [2, 16], replicated, may hold values from 0 to 511
- down_weight: bfloat16 [512, 8192, 16], P(None, ('tp', 'fsdp')), may hold values from -0.0625 to 0.0625
- up_weight: bfloat16 [512, 16, 2048], P(None, None, ('tp', 'fsdp')), may hold values from -0.125 to 0.125
Outputs:
- key_value_output: bfloat16 [2, 2048, 2048], P(None, 'fsdp', 'tp')
- input_gradient: bfloat16 [2, 2048, 8192], P(None, 'fsdp', 'tp')
- grad_down: float32 [512, 8192, 16], P(None, ('tp', 'fsdp'))
- up_weight_gradient: float32 [512, 16, 2048], P(None, None, ('tp', 'fsdp'))
Inputs may be any that keep to these rules, and one draw needn't show every extreme that they name: `block_adapter_index`: one adapter for each block of 128 rows of a microbatch.
All inputs are finite; a program needn't handle non-finite values.
Results may differ from a plain program's by a relative error of at most 0.005.
Values may be sent and summed in bfloat16 or wider, within the bound.
No kernel may reach another device: no remote copies, remote signals or barrier semaphores. Data moves between devices by JAX's collectives and lax.ppermute only.
A program may use at most 128 MiB of HBM per device.

v0:
```python
import functools

import jax
import jax.numpy as jnp
from jax import lax
from jax.experimental import pallas as pl
from jax.experimental.pallas import tpu as pltpu
from jax.sharding import PartitionSpec as P


BLOCK = 128
LANES = 128

adapter_scale = 2.0


ANYWHERE = pl.BlockSpec(memory_space=pl.ANY)
VMEM = pl.BlockSpec(memory_space=pltpu.VMEM)
SMEM = pl.BlockSpec(memory_space=pltpu.SMEM)
LIMIT = pltpu.CompilerParams(vmem_limit_bytes=34 * 1024 * 1024)

ROW_ROW = (((1,), (1,)), ((), ()))


def cost(flops, moved):
    return pl.CostEstimate(flops=flops, bytes_accessed=moved, transcendentals=0)


def dot(left, right, dims=(((1,), (0,)), ((), ()))):
    return lax.dot_general(left, right, dims, preferred_element_type=jnp.float32)


def one_hot(ids, count):
    lane = lax.broadcasted_iota(jnp.int32, (ids.shape[0], count), 1)
    return jnp.where(lane == ids, 1.0, 0.0).astype(jnp.bfloat16)


def send(value, axis, count, route):
    return lax.ppermute(value, axis, [(i, route(i)) for i in range(count)])


def first_kernel(start, half, place, weight, theirs, sem):
    other = pl.multiple_of((1 - place[0]) * half + start, LANES)
    copy = pltpu.make_async_copy(weight.at[pl.ds(other, theirs.shape[0]), :], theirs, sem)
    copy.start()
    copy.wait()


def prep_kernel(start, place, weight, tok, cot, mine, theirs, tok_out, cot_out, sems):
    half = mine.shape[0]
    columns = cot_out.shape[1]
    x, core = place[0], place[1]
    own = pl.multiple_of(x * half, LANES)
    other = pl.multiple_of((1 - x) * half, LANES)
    side = pl.multiple_of(core * columns, LANES)
    copies = [
        pltpu.make_async_copy(
            weight.at[pl.ds(other + start, half - start), :], theirs, sems.at[0]
        ),
        pltpu.make_async_copy(weight.at[pl.ds(own, half), :], mine, sems.at[1]),
        pltpu.make_async_copy(tok.at[:, pl.ds(other, half)], tok_out, sems.at[2]),
        pltpu.make_async_copy(cot.at[:, pl.ds(side, columns)], cot_out, sems.at[3]),
    ]
    for copy in copies:
        copy.start()
    for copy in copies:
        copy.wait()


def pair_kernel(start, place, mine, theirs, out):
    depth, width = theirs.shape
    own = pl.ds(pl.multiple_of(place[0] * width, LANES), width)
    other = pl.ds(pl.multiple_of((1 - place[0]) * width, LANES), width)
    out[:, own] = mine[pl.ds(start, depth), :]
    out[:, other] = theirs[...]


WHOLE, MINE, THEIRS = 0, 1, 2


def chunk_kernel(plan, array_count, has_kv, last, start, half, *refs):
    refs = list(refs)
    take = lambda n: [refs.pop(0) for _ in range(n)]
    (place,) = take(1)
    arrays = take(array_count)
    tok_all, tok_pair, cot_own, cot_part, cot_rest, back, down = take(7)
    kv_in, _ = take(2) if has_kv else (None, None)
    out, ig_pair = take(2)
    kv_out = take(2) if last else take(1)
    weight, tok, cot, finished, sem = refs[:5]
    rows = tok_all.shape[0]
    depth, total = weight.shape
    count = len(plan)
    width = total // count
    columns = cot_part.shape[1]
    x, core = place[count], place[count + 1]
    base = pl.multiple_of(x * half + start, LANES)
    lower = pl.ds(rows, rows)
    tok[pl.ds(0, rows), :] = tok_all[:, pl.ds(base, depth)]
    tok[lower, :] = tok_pair[:, pl.ds(start, depth)]
    for i, pieces in enumerate(plan):
        for array, offset, kind in pieces:
            wide = arrays[array].shape[1]
            shift = {WHOLE: 0, MINE: x * wide, THEIRS: (1 - x) * wide}[kind]
            target = pl.ds(pl.multiple_of(place[i] * width + shift, LANES), wide)
            weight[:, target] = arrays[array][pl.ds(offset, depth), :]
        at = pl.ds(pl.multiple_of(place[i] * width, LANES), width)
        part = dot(tok[...], weight[:, at])
        if has_kv:
            part = part + kv_in[:, at]
        if last:
            wide_kv, narrow_kv = refs[5:]
            slot = pl.ds(pl.multiple_of(lax.rem(place[i] * width, columns), LANES), width)
            where = lax.rem(lax.div(place[i] * width, columns) + core, 2)
            wide_kv[where, :, slot] = part
            narrow_kv[where, :, slot] = part.astype(narrow_kv.dtype)
        else:
            kv_out[0][:, at] = part
    if last:
        kv_out[0][...] = wide_kv[0]
        kv_out[1][...] = narrow_kv[1]
    cot[pl.ds(0, rows), :] = cot_own[...]
    cot[lower, pl.ds(pl.multiple_of(core * columns, LANES), columns)] = cot_part[...]
    cot[lower, pl.ds(pl.multiple_of((1 - core) * columns, LANES), columns)] = cot_rest[...]
    tile = min(2 * LANES, depth)
    blocks = back.shape[0] // BLOCK

    @pl.loop(0, depth // tile)
    def _(step):
        at = pl.multiple_of(step * tile, tile)
        wide = pl.ds(pl.multiple_of(base + step * tile, LANES), tile)
        part = dot(cot[...], weight[pl.ds(at, tile), :], ROW_ROW)
        ig_pair[:, pl.ds(at, tile)] = part[rows:].astype(ig_pair.dtype)
        for m in range(blocks):
            own = pl.ds(m * BLOCK, BLOCK)
            adapter = dot(back[own, :], down[m, :, wide])
            adapter = adapter.astype(jnp.bfloat16).astype(jnp.float32)
            both = part[m * BLOCK : (m + 1) * BLOCK] + adapter
            finished[own, pl.ds(at, tile)] = both.astype(finished.dtype)

    result = pltpu.make_async_copy(finished, out.at[:, pl.ds(base, depth)], sem)
    result.start()
    result.wait()


def chunk_product(
    place, plan, arrays, tok, tok_pair, cot, cot_part, cot_rest, back, down, kv, out, start, depth, last
):
    rows, half = tok_pair.shape
    total = cot.shape[1]
    operands = [place, *arrays, tok, tok_pair, cot, cot_part, cot_rest, back, down]
    specs = [SMEM] + [VMEM] * (len(arrays) + 7)
    aliases = {}
    if kv is not None:
        aliases[len(operands) + 1] = 0
        operands += [kv, out]
        specs += [VMEM, ANYWHERE]
    shapes = [
        jax.ShapeDtypeStruct((rows, 2 * half), jnp.bfloat16),
        jax.ShapeDtypeStruct((rows, depth), jnp.bfloat16),
    ]
    out_specs = [ANYWHERE, VMEM]
    if last:
        shapes.append(jax.ShapeDtypeStruct((2 * rows, total // 2), jnp.float32))
        shapes.append(jax.ShapeDtypeStruct((2 * rows, total // 2), jnp.bfloat16))
        out_specs += [VMEM, VMEM]
    else:
        shapes.append(jax.ShapeDtypeStruct((2 * rows, total), jnp.float32))
        out_specs.append(VMEM)
    return pl.pallas_call(
        functools.partial(chunk_kernel, plan, len(arrays), kv is not None, last, start, half),
        out_shape=tuple(shapes),
        in_specs=specs,
        out_specs=tuple(out_specs),
        input_output_aliases=aliases,
        scratch_shapes=[
            pltpu.VMEM((depth, total), jnp.bfloat16),
            pltpu.VMEM((2 * rows, depth), jnp.bfloat16),
            pltpu.VMEM((2 * rows, total), jnp.bfloat16),
            pltpu.VMEM((rows, depth), jnp.bfloat16),
            pltpu.SemaphoreType.DMA,
        ]
        + [pltpu.VMEM((2, 2 * rows, total // 2), kind) for kind in (jnp.float32, jnp.bfloat16) if last],
        cost_estimate=cost(8 * rows * depth * total, 2 * depth * total + 16 * rows * total),
        compiler_params=LIMIT,
    )(*operands)


def fetch_kernel(blocks, ids, ids_column, down, up, out, scratch, sems):
    devices, ranks = out.shape[0], down.shape[1]
    features = up.shape[0] // ranks
    copies = []
    for i in range(devices * blocks):
        copies.append(
            pltpu.make_async_copy(
                down.at[ids[i]],
                out.at[i // blocks, pl.ds(i % blocks * ranks, ranks), :],
                sems.at[i],
            )
        )
        copies[-1].start()
    count = up.shape[1]
    chosen = [one_hot(ids_column[pl.ds(m * devices, devices), :], count) for m in range(blocks)]
    for r in range(ranks):
        rows = up[pl.ds(r * features, features), :]
        scratch[:, r, :] = jnp.concatenate([dot(c, rows, ROW_ROW) for c in chosen], axis=1)
    lanes = blocks * features
    packed = scratch[...].astype(out.dtype)
    out[:, pl.ds(blocks * ranks, ranks), pl.ds(0, lanes)] = packed
    rest = out.shape[2] - lanes
    out[:, pl.ds(blocks * ranks, ranks), pl.ds(lanes, rest)] = jnp.zeros(
        (devices, ranks, rest), out.dtype
    )
    for copy in copies:
        copy.wait()


def project_kernel(blocks, core_ref, got, tok, cot, down_out, up_out, part):
    devices, ranks = got.shape[0], part.shape[1]
    width = got.shape[2]
    columns = up_out.shape[2]
    features = columns // devices
    at = pl.ds(pl.multiple_of(core_ref[0] * columns, LANES), columns)
    for m in range(blocks):
        for d in range(devices):
            down_out[m, :, pl.ds(d * width, width)] = got[d, pl.ds(m * ranks, ranks), :]
        lane = pl.ds(m * features, features)
        row = pl.ds(blocks * ranks, ranks)
        for d in range(0, devices, 2):
            up_out[m, :, pl.ds(d * features, 2 * features)] = jnp.concatenate(
                [got[d, row, lane], got[d + 1, row, lane]], axis=1
            )
        own = pl.ds(m * BLOCK, BLOCK)
        part[m] = dot(down_out[m], tok[own, :], ROW_ROW)
        part[blocks + m] = adapter_scale * dot(up_out[m], cot[own, at], ROW_ROW)


def tile_kernel(blocks, core_ref, part, other, tok, cot, out, low_out, back_out):
    devices, ranks, width = out.shape[0], part.shape[1], out.shape[2]
    columns = cot.shape[1] // 2
    features = columns // devices
    at = pl.ds(pl.multiple_of(core_ref[0] * columns, LANES), columns)
    summed = part[...] + other[...]
    ups = []
    for m in range(blocks):
        own = pl.ds(m * BLOCK, BLOCK)
        low = summed[m].astype(jnp.bfloat16)
        back = summed[blocks + m].astype(jnp.bfloat16)
        low_out[own, :] = jnp.transpose(summed[m]).astype(jnp.bfloat16)
        back_out[own, :] = jnp.transpose(summed[blocks + m]).astype(jnp.bfloat16)
        for d in range(devices):
            piece = dot(back, tok[own, pl.ds(d * width, width)])
            out[d, pl.ds(m * ranks, ranks), :] = piece.astype(out.dtype)
        ups.append(adapter_scale * dot(low, cot[own, at]))
    lanes = blocks * features
    for d in range(devices):
        piece = jnp.concatenate([u[:, d * features : (d + 1) * features] for u in ups], axis=1)
        out[d, pl.ds(blocks * ranks, ranks), pl.ds(0, lanes)] = piece.astype(out.dtype)
    rest = width - lanes
    out[:, pl.ds(blocks * ranks, ranks), pl.ds(lanes, rest)] = jnp.zeros(
        (devices, ranks, rest), out.dtype
    )


def spread_kernel(blocks, ids, ids_column, got, down_out, up_out, scratch):
    step = pl.program_id(0)
    many, ranks = down_out.shape[0], down_out.shape[1]
    devices = got.shape[0]
    down_out[...] = jnp.zeros(down_out.shape, down_out.dtype)
    for i in range(devices * blocks):
        where = ids[i] - step * many

        @pl.when((where >= 0) & (where < many))
        def _():
            tile = got[i // blocks, pl.ds(i % blocks * ranks, ranks), :].astype(jnp.float32)
            down_out[where] = down_out[where] + tile

    @pl.when(step == 0)
    def _():
        count = up_out.shape[1]
        features = up_out.shape[0] // ranks
        scratch[...] = got[:, pl.ds(blocks * ranks, ranks), pl.ds(0, blocks * features)].astype(
            jnp.float32
        )
        chosen = [one_hot(ids_column[pl.ds(m * devices, devices), :], count) for m in range(blocks)]
        for r in range(ranks):
            turned = jnp.transpose(scratch[:, r, :]).astype(jnp.bfloat16)
            total = 0.0
            for m in range(blocks):
                total = total + dot(turned[m * features : (m + 1) * features], chosen[m])
            up_out[pl.ds(r * features, features), :] = total


def kv_pair_kernel(keep, got, out):
    rows = out.shape[0]
    lower = pl.ds(rows, rows)
    out[...] = (keep[lower, :] + got[lower, :].astype(jnp.float32)).astype(out.dtype)


def kv_kernel(keep, core_got, pair_got, low, up, out):
    rows = out.shape[0]
    for m in range(rows // BLOCK):
        own = pl.ds(m * BLOCK, BLOCK)
        base = keep[own, :] + core_got[own, :].astype(jnp.float32)
        base = base + pair_got[own, :].astype(jnp.float32)
        adapter = adapter_scale * dot(low[own, :], up[m])
        adapter = adapter.astype(jnp.bfloat16).astype(jnp.float32)
        out[own, :] = (base + adapter).astype(out.dtype)


def rest_kernel(starts, half, *refs):
    count = len(starts)
    place, got, back, down, _, out = refs[0], refs[1 : 1 + count], *refs[1 + count : 5 + count]
    finished, factors, sems = refs[5 + count :]
    x = place[0]
    base = pl.multiple_of((1 - x) * half, LANES)
    load = pltpu.make_async_copy(down.at[:, :, pl.ds(base, half)], factors, sems.at[count])
    load.start()
    load.wait()
    copies = []
    for i, start in enumerate(starts):
        depth = got[i].shape[1]
        at = pl.ds(start, depth)
        for m in range(factors.shape[0]):
            own = pl.ds(m * BLOCK, BLOCK)
            adapter = dot(back[own, :], factors[m, :, at]).astype(jnp.bfloat16)
            both = got[i][own, :].astype(jnp.float32) + adapter.astype(jnp.float32)
            finished[own, at] = both.astype(finished.dtype)
        copies.append(
            pltpu.make_async_copy(
                finished.at[:, at],
                out.at[:, pl.ds(pl.multiple_of(base + start, LANES), depth)],
                sems.at[i],
            )
        )
        copies[-1].start()
    for copy in copies:
        copy.wait()


def paired(tokens, frozen_weight, cotangent, block_adapter_index, down_weight, up_weight):
    batches, batch_rows, shard = tokens.shape
    total = cotangent.shape[2]
    columns = total // 2
    rows = batches * batch_rows
    half = shard // 2
    tok = tokens.reshape(rows, shard)
    cot = cotangent.reshape(rows, total)
    adapters, down_rows, ranks = down_weight.shape
    features = up_weight.shape[2]
    per_device = batch_rows // BLOCK
    blocks = batches * per_device
    count = lax.axis_size("fsdp")
    layers = count // 4
    index = lax.axis_index("fsdp")
    core = lax.axis_index("tp")
    x, y, z = index % 2, (index // 2) % 2, index // 4
    bf16, f32 = jnp.bfloat16, jnp.float32
    shape = jax.ShapeDtypeStruct

    def move(axis, width, route, value):
        return send(value, axis, width, route)

    x_send = lambda v: move("fsdp", count, lambda i: i ^ 1, v)
    y_send = lambda v: move("fsdp", count, lambda i: i ^ 2, v)
    z_send = lambda v: move("fsdp", count, lambda i: (i + 4) % count, v)
    core_send = lambda v: move("tp", 2, lambda i: i ^ 1, v)

    chunks = ((0, half // 2), (half // 2, half // 2))
    block = frozen_weight.shape[1]
    here = jnp.stack([x, core]).astype(jnp.int32)
    split = chunks[1][0]
    theirs = [
        pl.pallas_call(
            functools.partial(first_kernel, 0, half),
            name="first",
            out_shape=shape((split, block), bf16),
            in_specs=[SMEM, ANYWHERE],
            out_specs=VMEM,
            scratch_shapes=[pltpu.SemaphoreType.DMA],
            cost_estimate=cost(0, 4 * split * block),
            compiler_params=LIMIT,
        )(here, frozen_weight)
    ]
    mine, later, tok_sent, cot_sent = pl.pallas_call(
        functools.partial(prep_kernel, split),
        name="prep",
        out_shape=(
            shape((half, block), bf16),
            shape((half - split, block), bf16),
            shape((rows, half), bf16),
            shape((rows, columns), bf16),
        ),
        in_specs=[SMEM, ANYWHERE, ANYWHERE, ANYWHERE],
        out_specs=(VMEM,) * 4,
        scratch_shapes=[pltpu.SemaphoreType.DMA((4,))],
        cost_estimate=cost(0, 4 * (2 * half * block + rows * (half + columns))),
        compiler_params=LIMIT,
    )(here, frozen_weight, tok, cot)
    theirs.append(later)
    mine_y = y_send(mine)
    tok_pair = x_send(tok_sent)
    cot_part = x_send(cot_sent)
    cot_rest = core_send(cot_part)
    held, theirs_y = [], []
    for c, (start, depth) in enumerate(chunks):
        got = x_send(theirs[c])
        held.append(
            pl.pallas_call(
                functools.partial(pair_kernel, start),
                out_shape=shape((depth, 2 * block), bf16),
                in_specs=[SMEM, VMEM, VMEM],
                out_specs=VMEM,
                cost_estimate=cost(0, 8 * depth * block),
                compiler_params=LIMIT,
            )(here, mine, got)
        )
        theirs_y.append(y_send(got))

    ids = (
        block_adapter_index.reshape(batches, count, per_device)
        .transpose(1, 0, 2)
        .reshape(count, blocks)
    )
    id_list = ids.reshape(-1)
    id_column = ids.T.reshape(-1, 1)

    def exchange(value):
        return lax.all_to_all(value, "fsdp", split_axis=0, concat_axis=0, tiled=True)

    packet = shape((count, (blocks + 1) * ranks, down_rows), bf16)
    packet_bytes = 2 * count * (blocks + 1) * ranks * down_rows
    parcel = pl.pallas_call(
        functools.partial(fetch_kernel, blocks),
        name="fetch",
        out_shape=packet,
        in_specs=[SMEM, VMEM, ANYWHERE, VMEM],
        out_specs=VMEM,
        scratch_shapes=[
            pltpu.VMEM((count, ranks, blocks * features), f32),
            pltpu.SemaphoreType.DMA((count * blocks,)),
        ],
        cost_estimate=cost(0, 4 * packet_bytes),
        compiler_params=LIMIT,
    )(
        id_list,
        id_column,
        down_weight.transpose(0, 2, 1),
        up_weight.transpose(1, 2, 0).reshape(ranks * features, adapters),
    )
    arrived = exchange(parcel)
    core_place = core.astype(jnp.int32).reshape(1)
    down_mine, up_mine, part = pl.pallas_call(
        functools.partial(project_kernel, blocks),
        name="project",
        out_shape=(
            shape((blocks, ranks, shard), bf16),
            shape((blocks, ranks, columns), bf16),
            shape((2 * blocks, ranks, BLOCK), f32),
        ),
        in_specs=[SMEM, VMEM, VMEM, VMEM],
        out_specs=(VMEM, VMEM, VMEM),
        cost_estimate=cost(2 * rows * ranks * (shard + columns), 2 * rows * (shard + total)),
        compiler_params=LIMIT,
    )(core_place, arrived, tok, cot)
    other = core_send(part)
    tiles, low_rank, back_rank = pl.pallas_call(
        functools.partial(tile_kernel, blocks),
        name="tiles",
        out_shape=(packet, shape((rows, ranks), bf16), shape((rows, ranks), bf16)),
        in_specs=[SMEM, VMEM, VMEM, VMEM, VMEM],
        out_specs=(VMEM, VMEM, VMEM),
        cost_estimate=cost(2 * rows * ranks * (shard + columns), 2 * rows * (shard + total)),
        compiler_params=LIMIT,
    )(core_place, part, other, tok, cot)
    owned = exchange(tiles)
    many = adapters // 8
    grad_down, grad_up = pl.pallas_call(
        functools.partial(spread_kernel, blocks),
        name="spread",
        grid=(adapters // many,),
        out_shape=(
            shape((adapters, ranks, down_rows), f32),
            shape((ranks * features, adapters), f32),
        ),
        in_specs=[SMEM, VMEM, VMEM],
        out_specs=(
            pl.BlockSpec((many, ranks, down_rows), lambda i: (i, 0, 0)),
            pl.BlockSpec((ranks * features, adapters), lambda i: (0, 0)),
        ),
        scratch_shapes=[pltpu.VMEM((count, ranks, blocks * features), f32)],
        cost_estimate=cost(0, 4 * adapters * ranks * (down_rows + features)),
        compiler_params=LIMIT,
    )(id_list, id_column, owned)

    kv = out = None
    got_pieces = []
    for c, ((start, depth), own) in enumerate(zip(chunks, held)):
        arrays = [own, mine_y, theirs_y[c]]
        plan = [((0, 0, WHOLE),), ((1, start, MINE), (2, 0, THEIRS))]
        places = [z * 2 + y, z * 2 + 1 - y]
        for step in range(1, layers):
            own = z_send(own)
            layer = (z - step) % layers
            places += [layer * 2 + y, layer * 2 + 1 - y]
            plan += [((len(arrays), 0, WHOLE),), ((len(arrays) + 1, 0, WHOLE),)]
            arrays += [own, y_send(own)]
        last = start + depth == half
        results = chunk_product(
            jnp.stack(places + [x, core]).astype(jnp.int32),
            tuple(plan),
            arrays,
            tok,
            tok_pair,
            cot,
            cot_part,
            cot_rest,
            back_rank,
            down_mine,
            kv,
            out,
            start,
            depth,
            last,
        )
        out, pair = results[:2]
        kv = results[2]
        got_pieces.append(x_send(pair))
    keep, other_columns = results[2:]
    core_got = core_send(other_columns)
    pair_sum = pl.pallas_call(
        kv_pair_kernel,
        name="kv_pair",
        out_shape=shape((rows, columns), bf16),
        in_specs=[VMEM, VMEM],
        out_specs=VMEM,
        cost_estimate=cost(0, 12 * rows * columns),
        compiler_params=LIMIT,
    )(keep, core_got)
    pair_got = x_send(pair_sum)
    key_value = pl.pallas_call(
        kv_kernel,
        name="kv_end",
        out_shape=shape((rows, columns), bf16),
        in_specs=[VMEM] * 5,
        out_specs=VMEM,
        cost_estimate=cost(2 * rows * ranks * columns, 12 * rows * columns),
        compiler_params=LIMIT,
    )(keep, core_got, pair_got, low_rank, up_mine)
    starts = tuple(start for start, _ in chunks)
    out = pl.pallas_call(
        functools.partial(rest_kernel, starts, half),
        name="rest",
        out_shape=shape((rows, shard), bf16),
        in_specs=[SMEM] + [VMEM] * (len(starts) + 1) + [ANYWHERE, ANYWHERE],
        out_specs=ANYWHERE,
        input_output_aliases={len(starts) + 3: 0},
        scratch_shapes=[
            pltpu.VMEM((rows, half), bf16),
            pltpu.VMEM((blocks, ranks, half), bf16),
            pltpu.SemaphoreType.DMA((len(starts) + 1,)),
        ],
        cost_estimate=cost(2 * rows * ranks * half, 4 * rows * half),
        compiler_params=LIMIT,
    )(x.astype(jnp.int32).reshape(1), *got_pieces, back_rank, down_mine, out)
    return (
        key_value.reshape(batches, batch_rows, columns),
        out.reshape(batches, batch_rows, shard),
        grad_down.transpose(0, 2, 1),
        grad_up.reshape(ranks, features, adapters).transpose(2, 0, 1),
    )


def selected_sum(adapter_selector, tiles):
    flat = tiles.reshape(tiles.shape[0], -1)
    return lax.dot_general(
        adapter_selector,
        flat,
        (((0,), (0,)), ((), ())),
        precision=lax.Precision.HIGHEST,
        preferred_element_type=jnp.float32,
    )


def plain(tokens, frozen_weight, cotangent, block_adapter_index, down_weight, up_weight):
    microbatch_list, token_block_rows, shard_width = tokens.shape
    kv_width = cotangent.shape[2]
    key_value_slice = kv_width // lax.axis_size("tp")
    row_total = microbatch_list * token_block_rows
    tok_matrix = tokens.reshape(row_total, shard_width)
    cot_matrix = cotangent.reshape(row_total, kv_width)
    adapter_number = down_weight.shape[0]
    rank_width = down_weight.shape[2]
    adapter_range = jnp.arange(adapter_number, dtype=jnp.int32)
    gathered = lax.all_gather(frozen_weight, "fsdp", axis=1, tiled=True)
    kv_partial = jnp.dot(tok_matrix, gathered, preferred_element_type=jnp.float32)
    frozen_key_value = lax.psum_scatter(kv_partial, "tp", scatter_dimension=1, tiled=True)
    frozen_input_gradient = lax.dot_general(
        cot_matrix, gathered, (((1,), (1,)), ((), ())), preferred_element_type=jnp.float32
    )
    cot_slab = lax.dynamic_slice_in_dim(
        cotangent, lax.axis_index("tp") * key_value_slice, key_value_slice, 2
    )
    fsdp_count = lax.axis_size("fsdp")
    per_dev = token_block_rows // BLOCK
    dest_ids = (
        block_adapter_index.reshape(microbatch_list, fsdp_count, per_dev)
        .transpose(1, 0, 2)
        .reshape(fsdp_count, microbatch_list * per_dev)
    )
    down_send = jnp.take(down_weight, dest_ids, axis=0).transpose(0, 1, 3, 2)
    up_send = jnp.take(up_weight, dest_ids, axis=0)
    down_mine, up_mine = (
        lax.all_to_all(down_send, "fsdp", split_axis=0, concat_axis=3, tiled=True),
        lax.all_to_all(up_send, "fsdp", split_axis=0, concat_axis=3, tiled=True),
    )
    down_mine = down_mine.reshape(microbatch_list, per_dev, rank_width, shard_width)
    up_mine = up_mine.reshape(microbatch_list, per_dev, rank_width, key_value_slice)
    tok_blocks = tokens.reshape(microbatch_list, per_dev, BLOCK, shard_width)
    gradient_blocks = cot_slab.reshape(microbatch_list, per_dev, BLOCK, key_value_slice)
    low_part = jnp.einsum(
        "mnbc,mnrc->mnbr", tok_blocks, down_mine, preferred_element_type=jnp.float32
    )
    partial_input_gradient = adapter_scale * jnp.einsum(
        "fsvj,fsyj->fsvy", gradient_blocks, up_mine, preferred_element_type=jnp.float32
    )
    low_sum, back_sum = lax.psum((low_part, partial_input_gradient), "tp")
    low_rank = low_sum.astype(jnp.bfloat16)
    rank_gradient = back_sum.astype(jnp.bfloat16)
    adapter_key_value = (
        adapter_scale
        * jnp.einsum("elui,elis->elus", low_rank, up_mine, preferred_element_type=jnp.float32)
    ).astype(jnp.bfloat16)
    adapter_input_gradient = jnp.einsum(
        "mnbr,mnrc->mnbc", rank_gradient, down_mine, preferred_element_type=jnp.float32
    ).astype(jnp.bfloat16)
    adapter_key_value = adapter_key_value.reshape(
        microbatch_list, token_block_rows, key_value_slice
    )
    adapter_input_gradient = adapter_input_gradient.reshape(
        microbatch_list, token_block_rows, shard_width
    )
    down_tiles = jnp.einsum(
        "mnbc,mnbr->mnrc", tok_blocks, rank_gradient, preferred_element_type=jnp.float32
    )
    up_weight_tiles = adapter_scale * jnp.einsum(
        "puai,puac->puic", low_rank, gradient_blocks, preferred_element_type=jnp.float32
    )
    down_tiles = down_tiles.reshape(microbatch_list * per_dev, rank_width, shard_width)
    up_weight_tiles = up_weight_tiles.reshape(
        microbatch_list * per_dev, rank_width, key_value_slice
    )
    down_owned, up_owned = (
        lax.all_to_all(
            down_tiles.astype(jnp.bfloat16), "fsdp", split_axis=2, concat_axis=0, tiled=True
        ).astype(down_tiles.dtype),
        lax.all_to_all(
            up_weight_tiles.astype(jnp.bfloat16), "fsdp", split_axis=2, concat_axis=0, tiled=True
        ).astype(up_weight_tiles.dtype),
    )
    owned_ids = dest_ids.reshape(-1)
    adapter_selector = (owned_ids[:, None] == adapter_range[None, :]).astype(jnp.float32)
    grad_down = (
        selected_sum(adapter_selector, down_owned)
        .reshape(adapter_number, rank_width, down_weight.shape[1])
        .transpose(0, 2, 1)
    )
    up_weight_gradient = selected_sum(adapter_selector, up_owned).reshape(up_weight.shape)
    key_value_output = (
        frozen_key_value.reshape(microbatch_list, token_block_rows, key_value_slice)
        + adapter_key_value.astype(jnp.float32)
    ).astype(jnp.bfloat16)
    input_gradient = (
        frozen_input_gradient.reshape(microbatch_list, token_block_rows, shard_width)
        + adapter_input_gradient.astype(jnp.float32)
    ).astype(jnp.bfloat16)
    return (key_value_output, input_gradient, grad_down, up_weight_gradient)


def local(tokens, frozen_weight, cotangent, block_adapter_index, down_weight, up_weight):
    batches, batch_rows, shard = tokens.shape
    blocks = batches * (batch_rows // BLOCK)
    features = up_weight.shape[2]
    fits = (
        lax.axis_size("tp") == 2
        and lax.axis_size("fsdp") % 4 == 0
        and frozen_weight.shape[1] % LANES == 0
        and shard % (16 * 2 * LANES) == 0
        and blocks * features == LANES
        and 2 * features == LANES
        and down_weight.shape[1] > LANES
        and down_weight.shape[0] % (8 * LANES // 2) == 0
    )
    body = paired if fits else plain
    return body(tokens, frozen_weight, cotangent, block_adapter_index, down_weight, up_weight)


def solution(mesh):
    return jax.shard_map(
        local,
        mesh=mesh,
        in_specs=(
            P(None, "fsdp", "tp"),
            P("tp", "fsdp"),
            P(None, "fsdp", None),
            P(),
            P(None, ("tp", "fsdp"), None),
            P(None, None, ("tp", "fsdp")),
        ),
        out_specs=(
            P(None, "fsdp", "tp"),
            P(None, "fsdp", "tp"),
            P(None, ("tp", "fsdp"), None),
            P(None, None, ("tp", "fsdp")),
        ),
        check_vma=False,
    )
```

profile of v0, /device:TPU:0, one launch (start us, length us, event | category | flops | bytes accessed | tf_op | source)
XLA Modules:
  0.0 221.8 jit_solution(15799504199209595450)
XLA Ops:
  0.7 1.2 copy-done.7
  2.5 3.0 %collective-permute-start.13 = (bf16[1024,128]{1,0:T(8,128)(2,1)S(1)}, bf16[1024,128]{1,0:T(8,128)(2,1)}, u32[]{:S(2)}, u32[]{:S(2)}) collective-permute-start(bf16[1024,128]{1,0:T(8,128)(2,1)S(1)} %first.1), channel_id=1, source_target_pairs={{0,2},{2,0},{4,6},{6,4},{8,10},{10,8},{12,14},{14,12},{16,18},{18,... | collective-permute-start | bytes 786440 | tf_op jit(solution)/shard_map/ppermute | solution.py:39
  5.6 1.6 copy-done
  7.2 1.2 copy-done.2
  8.4 1.6 prep.1
  10.0 2.0 collective-permute-done.13.theirs
  12.0 1.0 shard_map.94.refs_1_
  13.0 1.9 collective-permute-start.15
  14.9 1.5 collective-permute-start
  16.4 5.4 %collective-permute-done.theirs = bf16[1024,128]{1,0:T(8,128)(2,1)S(1)} collective-permute-done((bf16[1024,128]{1,0:T(8,128)(2,1)S(1)}, bf16[1024,128]{1,0:T(8,128)(2,1)S(1)}, u32[]{:S(2)}, u32[]{:S(2)}) %collective-permute-start) | collective-permute-done | bytes 262176 | tf_op jit(solution)/shard_map/ppermute | solution.py:39
  21.8 1.4 shard_map.93.refs_1_
  23.3 1.6 collective-permute-start.3
  24.8 1.5 collective-permute-start.10
  26.3 3.5 %collective-permute-done.15.refs_4_ = bf16[1024,256]{1,0:T(8,128)(2,1)} collective-permute-done((bf16[1024,256]{1,0:T(8,128)(2,1)S(1)}, bf16[1024,256]{1,0:T(8,128)(2,1)}, u32[]{:S(2)}, u32[]{:S(2)}) %collective-permute-start.15) | collective-permute-done | bytes 524320 | tf_op jit(solution)/shard_map/ppermute | solution.py:39
  29.8 1.7 collective-permute-start.14
  31.9 2.2 copy-done.8
  34.1 1.2 copy-done.13
  35.3 2.9 %fetch.1 = bf16[16,48,256]{2,1,0:T(8,128)(2,1)} custom-call(s32[32]{0:T(128)S(1)} %reshape_reshape.3.ids, s32[32,1]{1,0:T(8,128)S(1)} %reshape.43.ids_column, bf16[512,16,256]{2,1,0:T(8,128)(2,1)S(1)} %bitcast.37, bf16[1024,512]{1,0:T(8,128)(2,1)S(1)} %bitcast.38), custom_call_target="tpu_custom_call" | custom-call | bytes 1572864 | tf_op jit(solution)/shard_map/fetch/pallas_call | solution.py:433
  38.2 6.1 %all-to-all-start = ((bf16[16,48,256]{2,1,0:T(8,128)(2,1)}), bf16[16,48,256]{2,1,0:T(8,128)(2,1)S(1)}, u32[]{:S(2)}, u32[]{:S(2)}) async-start(bf16[16,48,256]{2,1,0:T(8,128)(2,1)} %fetch.1), calls=%async_computation | async-start | bytes 786432 | tf_op jit(solution)/shard_map/all_to_all | solution.py:429
  44.3 1.9 collective-permute-start.1
  46.3 1.5 collective-permute-start.9
  47.7 1.5 collective-permute-start.5
  49.2 3.2 %collective-permute-done.17.refs_6_ = bf16[1024,256]{1,0:T(8,128)(2,1)} collective-permute-done((bf16[1024,256]{1,0:T(8,128)(2,1)}, bf16[1024,256]{1,0:T(8,128)(2,1)}, u32[]{:S(2)}, u32[]{:S(2)}) %collective-permute-start.17) | collective-permute-done | bytes 524320 | tf_op jit(solution)/shard_map/ppermute | solution.py:39
  52.4 1.7 collective-permute-start.19
  54.1 27.7 %all-to-all-done.got = bf16[16,48,256]{2,1,0:T(8,128)(2,1)S(1)} async-done(((bf16[16,48,256]{2,1,0:T(8,128)(2,1)}), bf16[16,48,256]{2,1,0:T(8,128)(2,1)S(1)}, u32[]{:S(2)}, u32[]{:S(2)}) %all-to-all-start) | async-done | bytes 393248 | tf_op jit(solution)/shard_map/all_to_all | solution.py:429
  85.2 1.1 collective-permute-start.16
  86.3 1.5 collective-permute-start.7
  87.8 1.0 collective-permute-start.18
  89.9 1.0 collective-permute-start.4
  90.9 9.3 %collective-permute-done.16.refs_5_ = bf16[1024,256]{1,0:T(8,128)(2,1)S(1)} collective-permute-done((bf16[1024,256]{1,0:T(8,128)(2,1)}, bf16[1024,256]{1,0:T(8,128)(2,1)S(1)}, u32[]{:S(2)}, u32[]{:S(2)}) %collective-permute-start.16) | collective-permute-done | bytes 524320 | tf_op jit(solution)/shard_map/ppermute | solution.py:39
  101.0 1.1 collective-permute-start.6
  105.1 6.5 %collective-permute-done.18.refs_7_ = bf16[1024,256]{1,0:T(8,128)(2,1)} collective-permute-done((bf16[1024,256]{1,0:T(8,128)(2,1)}, bf16[1024,256]{1,0:T(8,128)(2,1)}, u32[]{:S(2)}, u32[]{:S(2)}) %collective-permute-start.18) | collective-permute-done | bytes 524320 | tf_op jit(solution)/shard_map/ppermute | solution.py:39
  111.6 1.1 collective-permute-start.2
  112.7 10.1 %collective-permute-done.20.refs_9_ = bf16[1024,256]{1,0:T(8,128)(2,1)} collective-permute-done((bf16[1024,256]{1,0:T(8,128)(2,1)}, bf16[1024,256]{1,0:T(8,128)(2,1)}, u32[]{:S(2)}, u32[]{:S(2)}) %collective-permute-start.20) | collective-permute-done | bytes 524320 | tf_op jit(solution)/shard_map/ppermute | solution.py:39
  122.8 9.9 %shard_map.95 = (bf16[256,4096]{1,0:T(8,128)(2,1)}, bf16[256,1024]{1,0:T(8,128)(2,1)S(1)}, f32[512,2048]{1,0:T(8,128)S(1)}) custom-call(s32[10]{0:T(128)S(1)} %stack.59.refs_0_, bf16[1024,256]{1,0:T(8,128)(2,1)S(1)} %copy-done.15, bf16[2048,128]{1,0:T(8,128)(2,1)} %collective-permute-done.1.refs_2_, bf16[1024,128]{1,0:T(8,128)(2,1)} %collective-permute-done.14.refs_3_, ...), custom_call_target="tpu_custom_call" | custom-call | flops 4294967296 | bytes 12582912 | tf_op jit(solution)/shard_map/pallas_call | solution.py:170
  132.7 28.5 %collective-permute-done.2.refs_3_ = bf16[1024,128]{1,0:T(8,128)(2,1)S(1)} collective-permute-done((bf16[1024,128]{1,0:T(8,128)(2,1)S(1)}, bf16[1024,128]{1,0:T(8,128)(2,1)S(1)}, u32[]{:S(2)}, u32[]{:S(2)}) %collective-permute-start.2) | collective-permute-done | bytes 262176 | tf_op jit(solution)/shard_map/ppermute | solution.py:39
  161.2 11.5 %shard_map.96 = (bf16[256,4096]{1,0:T(8,128)(2,1)}, bf16[256,1024]{1,0:T(8,128)(2,1)S(1)}, f32[512,1024]{1,0:T(8,128)S(1)}, bf16[512,1024]{1,0:T(8,128)(2,1)}) custom-call(s32[10]{0:T(128)S(1)} %stack.59.refs_0_, bf16[1024,256]{1,0:T(8,128)(2,1)} %shard_map.93.refs_1_, ...), custom_call_target="tpu_custom_call", output_to_operand_aliasing={{0}: (18, {})} | custom-call | flops 4294967296 | bytes 12582912 | tf_op jit(solution)/shard_map/pallas_call | solution.py:170
  172.8 1.3 copy-done.4
  174.9 3.6 %all-to-all-start.1 = ((bf16[16,48,256]{2,1,0:T(8,128)(2,1)}), bf16[16,48,256]{2,1,0:T(8,128)(2,1)S(1)}, u32[]{:S(2)}, u32[]{:S(2)}) async-start(bf16[16,48,256]{2,1,0:T(8,128)(2,1)} %copy-done.16), calls=%async_computation.1 | async-start | bytes 786432 | tf_op jit(solution)/shard_map/all_to_all | solution.py:429
  178.5 1.8 collective-permute-start.24
  180.6 1.6 copy-done.5
  183.0 1.7 collective-permute-start.22
  184.8 6.8 %all-to-all-done.1.got = bf16[16,48,256]{2,1,0:T(8,128)(2,1)S(1)} async-done(((bf16[16,48,256]{2,1,0:T(8,128)(2,1)}), bf16[16,48,256]{2,1,0:T(8,128)(2,1)S(1)}, u32[]{:S(2)}, u32[]{:S(2)}) %all-to-all-start.1) | async-done | bytes 393248 | tf_op jit(solution)/shard_map/all_to_all | solution.py:429
  192.3 7.8 %spread.1 = (f32[512,16,256]{2,1,0:T(8,128)}, f32[1024,512]{1,0:T(8,128)}) custom-call(s32[32]{0:T(128)S(1)} %copy-done.28, s32[32,1]{1,0:T(8,128)S(1)} %reshape.43.ids_column, bf16[16,48,256]{2,1,0:T(8,128)(2,1)S(1)} %all-to-all-done.1.got), custom_call_target="tpu_custom_call" | custom-call | bytes 10485760 | tf_op jit(solution)/shard_map/spread/pallas_call | solution.py:478
  200.1 8.8 %collective-permute-done.23.refs_1_ = bf16[256,1024]{1,0:T(8,128)(2,1)} collective-permute-done((bf16[256,1024]{1,0:T(8,128)(2,1)}, bf16[256,1024]{1,0:T(8,128)(2,1)}, u32[]{:S(2)}, u32[]{:S(2)}) %collective-permute-start.23) | collective-permute-done | bytes 524320 | tf_op jit(solution)/shard_map/ppermute | solution.py:39
  210.6 2.6 %rest.1 = bf16[256,4096]{1,0:T(8,128)(2,1)} custom-call(s32[1]{0:T(128)} %bitcast.8.refs_0_, bf16[256,1024]{1,0:T(8,128)(2,1)} %collective-permute-done.23.refs_1_, bf16[256,1024]{1,0:T(8,128)(2,1)} %collective-permute-done.24.refs_2_, bf16[256,16]{1,0:T(8,128)(2,1)S(1)} %copy-done.18, ...), custom_call_target="tpu_custom_call", output_to_operand_aliasing={{}: (5, {})} | custom-call | flops 16777216 | bytes 2097152 | tf_op jit(solution)/shard_map/rest/pallas_call | solution.py:551
  213.3 6.3 %collective-permute-done.22.pair_got = bf16[256,1024]{1,0:T(8,128)(2,1)} collective-permute-done((bf16[256,1024]{1,0:T(8,128)(2,1)}, bf16[256,1024]{1,0:T(8,128)(2,1)}, u32[]{:S(2)}, u32[]{:S(2)}) %collective-permute-start.22) | collective-permute-done | bytes 524320 | tf_op jit(solution)/shard_map/ppermute | solution.py:39
  219.6 2.2 kv_end.1
  (94 shorter events, 13.5 us)
Async XLA Ops:
  2.5 9.4 %collective-permute-start.13 = (bf16[1024,128]{1,0:T(8,128)(2,1)S(1)}, bf16[1024,128]{1,0:T(8,128)(2,1)}, u32[]{:S(2)}, u32[]{:S(2)}) collective-permute-start(bf16[1024,128]{1,0:T(8,128)(2,1)S(1)} %first.1), channel_id=1, source_target_pairs={{0,2},{2,0},{4,6},{6,4},{8,10},{10,8},{12,14},{14,12},{16,18},{18,... | collective-permute-start | bytes 786440 | tf_op jit(solution)/shard_map/ppermute | solution.py:39
  5.6 1.6 copy-start
  10.0 11.8 %copy-start.9 = (bf16[2048,128]{1,0:T(8,128)(2,1)}, bf16[2048,128]{1,0:T(8,128)(2,1)S(1)}, u32[]{:S(2)}) copy-start(bf16[2048,128]{1,0:T(8,128)(2,1)S(1)} %get-tuple-element.23.mine) | copy-start | bytes 1572868
  10.0 19.8 %copy-start.29 = (bf16[256,2048]{1,0:T(8,128)(2,1)}, bf16[256,2048]{1,0:T(8,128)(2,1)S(1)}, u32[]{:S(2)}) copy-start(bf16[256,2048]{1,0:T(8,128)(2,1)S(1)} %get-tuple-element.25) | copy-start | bytes 3145732
  10.0 21.6 %copy-start.34 = (s32[2,16]{1,0:T(2,128)S(1)}, s32[2,16]{1,0:T(2,128)}, u32[]{:S(2)}) copy-start(s32[2,16]{1,0:T(2,128)} %param.9) | copy-start | bytes 388
  13.0 18.8 %copy-start.14 = (bf16[1024,256]{1,0:T(8,128)(2,1)}, bf16[1024,256]{1,0:T(8,128)(2,1)S(1)}, u32[]{:S(2)}) copy-start(bf16[1024,256]{1,0:T(8,128)(2,1)S(1)} %shard_map.94.refs_1_) | copy-start | bytes 1572868
  13.0 16.8 %collective-permute-start.15 = (bf16[1024,256]{1,0:T(8,128)(2,1)S(1)}, bf16[1024,256]{1,0:T(8,128)(2,1)}, u32[]{:S(2)}, u32[]{:S(2)}) collective-permute-start(bf16[1024,256]{1,0:T(8,128)(2,1)S(1)} %shard_map.94.refs_1_), channel_id=1, source_target_pairs={{0,8},{2,10},{4,12},{6,14},{8,16},{10,18},{12,20},{14,22},{16,24},... | collective-permute-start | bytes 1572872 | tf_op jit(solution)/shard_map/ppermute | solution.py:39
  14.9 6.9 %collective-permute-start = (bf16[1024,128]{1,0:T(8,128)(2,1)S(1)}, bf16[1024,128]{1,0:T(8,128)(2,1)S(1)}, u32[]{:S(2)}, u32[]{:S(2)}) collective-permute-start(bf16[1024,128]{1,0:T(8,128)(2,1)S(1)} %get-tuple-element.24), channel_id=1, source_target_pairs={{0,2},{2,0},{4,6},{6,4},{8,10},{10,8},{12,14},{14,12},{16,18},{18,... | collective-permute-start | bytes 786440 | tf_op jit(solution)/shard_map/ppermute | solution.py:39
  21.8 10.0 %copy-start.19 = (bf16[1024,128]{1,0:T(8,128)(2,1)}, bf16[1024,128]{1,0:T(8,128)(2,1)S(1)}, u32[]{:S(2)}) copy-start(bf16[1024,128]{1,0:T(8,128)(2,1)S(1)} %collective-permute-done.theirs) | copy-start | bytes 786436
  23.3 24.5 %collective-permute-start.3 = (bf16[1024,256]{1,0:T(8,128)(2,1)}, bf16[1024,256]{1,0:T(8,128)(2,1)}, u32[]{:S(2)}, u32[]{:S(2)}) collective-permute-start(bf16[1024,256]{1,0:T(8,128)(2,1)} %shard_map.93.refs_1_), channel_id=1, source_target_pairs={{0,8},{2,10},{4,12},{6,14},{8,16},{10,18},{12,20},{14,22},{16,24},... | collective-permute-start | bytes 1572872 | tf_op jit(solution)/shard_map/ppermute | solution.py:39
  24.8 24.4 %collective-permute-start.10 = (bf16[256,1024]{1,0:T(8,128)(2,1)}, bf16[256,1024]{1,0:T(8,128)(2,1)}, u32[]{:S(2)}, u32[]{:S(2)}) collective-permute-start(bf16[256,1024]{1,0:T(8,128)(2,1)} %get-tuple-element.26), channel_id=1, source_target_pairs={{0,2},{2,0},{4,6},{6,4},{8,10},{10,8},{12,14},{14,12},{16,18},{18,... | collective-permute-start | bytes 1572872 | tf_op jit(solution)/shard_map/ppermute | solution.py:39
  29.8 22.6 %collective-permute-start.17 = (bf16[1024,256]{1,0:T(8,128)(2,1)}, bf16[1024,256]{1,0:T(8,128)(2,1)}, u32[]{:S(2)}, u32[]{:S(2)}) collective-permute-start(bf16[1024,256]{1,0:T(8,128)(2,1)} %collective-permute-done.15.refs_4_), channel_id=1, source_target_pairs={{0,8},{2,10},{4,12},{6,14},{8,16},{10,18},{12,20},{14,22},{16,24},... | collective-permute-start | bytes 1572872 | tf_op jit(solution)/shard_map/ppermute | solution.py:39
  29.8 16.4 %collective-permute-start.14 = (bf16[1024,128]{1,0:T(8,128)(2,1)}, bf16[1024,128]{1,0:T(8,128)(2,1)}, u32[]{:S(2)}, u32[]{:S(2)}) collective-permute-start(bf16[1024,128]{1,0:T(8,128)(2,1)} %collective-permute-done.13.theirs), channel_id=1, source_target_pairs={{0,4},{2,6},{4,0},{6,2},{8,12},{10,14},{12,8},{14,10},{16,20},{18,... | collective-permute-start | bytes 786440 | tf_op jit(solution)/shard_map/ppermute | solution.py:39
  31.8 6.3 %copy-start.27 = (s32[32]{0:T(128)}, s32[32]{0:T(128)S(1)}, u32[]{:S(2)}) copy-start(s32[32]{0:T(128)S(1)} %reshape_reshape.3.ids) | copy-start | bytes 388
  31.9 2.2 copy-start.8
  35.3 46.5 %copy-start.1 = (bf16[2,128,4096]{2,1,0:T(8,128)(2,1)S(1)}, bf16[2,128,4096]{2,1,0:T(8,128)(2,1)}, u32[]{:S(2)}) copy-start(bf16[2,128,4096]{2,1,0:T(8,128)(2,1)} %param.6) | copy-start | bytes 6291460
  35.3 46.5 %copy-start.3 = (bf16[2,128,2048]{2,1,0:T(8,128)(2,1)S(1)}, bf16[2,128,2048]{2,1,0:T(8,128)(2,1)}, u32[]{:S(2)}) copy-start(bf16[2,128,2048]{2,1,0:T(8,128)(2,1)} %param.8) | copy-start | bytes 3145732
  38.2 43.6 %all-to-all-start = ((bf16[16,48,256]{2,1,0:T(8,128)(2,1)}), bf16[16,48,256]{2,1,0:T(8,128)(2,1)S(1)}, u32[]{:S(2)}, u32[]{:S(2)}) async-start(bf16[16,48,256]{2,1,0:T(8,128)(2,1)} %fetch.1), calls=%async_computation | async-start | bytes 786432 | tf_op jit(solution)/shard_map/all_to_all | solution.py:429
  44.3 39.7 %collective-permute-start.1 = (bf16[2048,128]{1,0:T(8,128)(2,1)}, bf16[2048,128]{1,0:T(8,128)(2,1)}, u32[]{:S(2)}, u32[]{:S(2)}) collective-permute-start(bf16[2048,128]{1,0:T(8,128)(2,1)} %copy-done.9), channel_id=1, source_target_pairs={{0,4},{2,6},{4,0},{6,2},{8,12},{10,14},{12,8},{14,10},{16,20},{18,... | collective-permute-start | bytes 1572872 | tf_op jit(solution)/shard_map/ppermute | solution.py:39
  46.3 43.6 %collective-permute-start.9 = (bf16[256,2048]{1,0:T(8,128)(2,1)}, bf16[256,2048]{1,0:T(8,128)(2,1)}, u32[]{:S(2)}, u32[]{:S(2)}) collective-permute-start(bf16[256,2048]{1,0:T(8,128)(2,1)} %copy-done.29), channel_id=1, source_target_pairs={{0,2},{2,0},{4,6},{6,4},{8,10},{10,8},{12,14},{14,12},{16,18},{18,... | collective-permute-start | bytes 3145736 | tf_op jit(solution)/shard_map/ppermute | solution.py:39
  47.7 38.6 %collective-permute-start.5 = (bf16[1024,256]{1,0:T(8,128)(2,1)}, bf16[1024,256]{1,0:T(8,128)(2,1)}, u32[]{:S(2)}, u32[]{:S(2)}) collective-permute-start(bf16[1024,256]{1,0:T(8,128)(2,1)} %collective-permute-done.3.refs_4_), channel_id=1, source_target_pairs={{0,8},{2,10},{4,12},{6,14},{8,16},{10,18},{12,20},{14,22},{16,24},... | collective-permute-start | bytes 1572872 | tf_op jit(solution)/shard_map/ppermute | solution.py:39
  49.2 38.6 %collective-permute-start.11 = (bf16[256,1024]{1,0:T(8,128)(2,1)}, bf16[256,1024]{1,0:T(8,128)(2,1)}, u32[]{:S(2)}, u32[]{:S(2)}) collective-permute-start(bf16[256,1024]{1,0:T(8,128)(2,1)} %collective-permute-done.10.refs_13_), channel_id=1, source_target_pairs={{0,1},{1,0},{2,3},{3,2},{4,5},{5,4},{6,7},{7,6},{8,9},{9,8},{10,11... | collective-permute-start | bytes 1572872 | tf_op jit(solution)/shard_map/ppermute | solution.py:39
  52.4 36.5 %collective-permute-start.19 = (bf16[1024,256]{1,0:T(8,128)(2,1)}, bf16[1024,256]{1,0:T(8,128)(2,1)}, u32[]{:S(2)}, u32[]{:S(2)}) collective-permute-start(bf16[1024,256]{1,0:T(8,128)(2,1)} %collective-permute-done.17.refs_6_), channel_id=1, source_target_pairs={{0,8},{2,10},{4,12},{6,14},{8,16},{10,18},{12,20},{14,22},{16,24},... | collective-permute-start | bytes 1572872 | tf_op jit(solution)/shard_map/ppermute | solution.py:39
  84.0 38.8 %copy-start.11 = (bf16[2,16,4096]{2,1,0:T(8,128)(2,1)S(1)}, bf16[2,16,4096]{2,1,0:T(8,128)(2,1)}, u32[]{:S(2)}) copy-start(bf16[2,16,4096]{2,1,0:T(8,128)(2,1)} %copy-done.10) | copy-start | bytes 786436
  84.0 1.2 collective-permute-start.12
  85.2 15.0 %collective-permute-start.16 = (bf16[1024,256]{1,0:T(8,128)(2,1)}, bf16[1024,256]{1,0:T(8,128)(2,1)S(1)}, u32[]{:S(2)}, u32[]{:S(2)}) collective-permute-start(bf16[1024,256]{1,0:T(8,128)(2,1)} %collective-permute-done.15.refs_4_), channel_id=1, source_target_pairs={{0,4},{2,6},{4,0},{6,2},{8,12},{10,14},{12,8},{14,10},{16,20},{18,... | collective-permute-start | bytes 1572872 | tf_op jit(solution)/shard_map/ppermute | solution.py:39
  86.3 15.8 %collective-permute-start.7 = (bf16[1024,256]{1,0:T(8,128)(2,1)}, bf16[1024,256]{1,0:T(8,128)(2,1)}, u32[]{:S(2)}, u32[]{:S(2)}) collective-permute-start(bf16[1024,256]{1,0:T(8,128)(2,1)} %collective-permute-done.5.refs_6_), channel_id=1, source_target_pairs={{0,8},{2,10},{4,12},{6,14},{8,16},{10,18},{12,20},{14,22},{16,24},... | collective-permute-start | bytes 1572872 | tf_op jit(solution)/shard_map/ppermute | solution.py:39
  87.8 23.7 %collective-permute-start.18 = (bf16[1024,256]{1,0:T(8,128)(2,1)}, bf16[1024,256]{1,0:T(8,128)(2,1)}, u32[]{:S(2)}, u32[]{:S(2)}) collective-permute-start(bf16[1024,256]{1,0:T(8,128)(2,1)} %collective-permute-done.17.refs_6_), channel_id=1, source_target_pairs={{0,4},{2,6},{4,0},{6,2},{8,12},{10,14},{12,8},{14,10},{16,20},{18,... | collective-permute-start | bytes 1572872 | tf_op jit(solution)/shard_map/ppermute | solution.py:39
  88.9 33.9 %collective-permute-start.20 = (bf16[1024,256]{1,0:T(8,128)(2,1)}, bf16[1024,256]{1,0:T(8,128)(2,1)}, u32[]{:S(2)}, u32[]{:S(2)}) collective-permute-start(bf16[1024,256]{1,0:T(8,128)(2,1)} %collective-permute-done.19.refs_8_), channel_id=1, source_target_pairs={{0,4},{2,6},{4,0},{6,2},{8,12},{10,14},{12,8},{14,10},{16,20},{18,... | collective-permute-start | bytes 1572872 | tf_op jit(solution)/shard_map/ppermute | solution.py:39
  89.9 71.3 %collective-permute-start.4 = (bf16[1024,256]{1,0:T(8,128)(2,1)}, bf16[1024,256]{1,0:T(8,128)(2,1)}, u32[]{:S(2)}, u32[]{:S(2)}) collective-permute-start(bf16[1024,256]{1,0:T(8,128)(2,1)} %collective-permute-done.3.refs_4_), channel_id=1, source_target_pairs={{0,4},{2,6},{4,0},{6,2},{8,12},{10,14},{12,8},{14,10},{16,20},{18,... | collective-permute-start | bytes 1572872 | tf_op jit(solution)/shard_map/ppermute | solution.py:39
  101.0 60.2 %collective-permute-start.6 = (bf16[1024,256]{1,0:T(8,128)(2,1)}, bf16[1024,256]{1,0:T(8,128)(2,1)}, u32[]{:S(2)}, u32[]{:S(2)}) collective-permute-start(bf16[1024,256]{1,0:T(8,128)(2,1)} %collective-permute-done.5.refs_6_), channel_id=1, source_target_pairs={{0,4},{2,6},{4,0},{6,2},{8,12},{10,14},{12,8},{14,10},{16,20},{18,... | collective-permute-start | bytes 1572872 | tf_op jit(solution)/shard_map/ppermute | solution.py:39
  102.1 59.1 %collective-permute-start.8 = (bf16[1024,256]{1,0:T(8,128)(2,1)}, bf16[1024,256]{1,0:T(8,128)(2,1)}, u32[]{:S(2)}, u32[]{:S(2)}) collective-permute-start(bf16[1024,256]{1,0:T(8,128)(2,1)} %collective-permute-done.7.refs_8_), channel_id=1, source_target_pairs={{0,4},{2,6},{4,0},{6,2},{8,12},{10,14},{12,8},{14,10},{16,20},{18,... | collective-permute-start | bytes 1572872 | tf_op jit(solution)/shard_map/ppermute | solution.py:39
  103.9 7.6 %copy-start.20 = (bf16[1024,128]{1,0:T(8,128)(2,1)S(1)}, bf16[1024,128]{1,0:T(8,128)(2,1)}, u32[]{:S(2)}) copy-start(bf16[1024,128]{1,0:T(8,128)(2,1)} %copy-done.19) | copy-start | bytes 786436
  103.9 18.9 %copy-start.15 = (bf16[1024,256]{1,0:T(8,128)(2,1)S(1)}, bf16[1024,256]{1,0:T(8,128)(2,1)}, u32[]{:S(2)}) copy-start(bf16[1024,256]{1,0:T(8,128)(2,1)} %copy-done.14) | copy-start | bytes 1572868
  103.9 18.9 %copy-start.31 = (bf16[1024,256]{1,0:T(8,128)(2,1)S(1)}, bf16[1024,256]{1,0:T(8,128)(2,1)}, u32[]{:S(2)}) copy-start(bf16[1024,256]{1,0:T(8,128)(2,1)} %copy-done.30) | copy-start | bytes 1572868
  105.1 17.7 %copy-start.16 = (bf16[16,48,256]{2,1,0:T(8,128)(2,1)}, bf16[16,48,256]{2,1,0:T(8,128)(2,1)S(1)}, u32[]{:S(2)}) copy-start(bf16[16,48,256]{2,1,0:T(8,128)(2,1)S(1)} %get-tuple-element.39) | copy-start | bytes 1179652
  105.1 56.2 %copy-start.17 = (bf16[256,16]{1,0:T(8,128)(2,1)}, bf16[256,16]{1,0:T(8,128)(2,1)S(1)}, u32[]{:S(2)}) copy-start(bf16[256,16]{1,0:T(8,128)(2,1)S(1)} %get-tuple-element.28.refs_15_.refs_3_) | copy-start | bytes 24580
  111.6 49.6 %collective-permute-start.2 = (bf16[1024,128]{1,0:T(8,128)(2,1)S(1)}, bf16[1024,128]{1,0:T(8,128)(2,1)S(1)}, u32[]{:S(2)}, u32[]{:S(2)}) collective-permute-start(bf16[1024,128]{1,0:T(8,128)(2,1)S(1)} %copy-done.20), channel_id=1, source_target_pairs={{0,4},{2,6},{4,0},{6,2},{8,12},{10,14},{12,8},{14,10},{16,20},{18,... | collective-permute-start | bytes 786440 | tf_op jit(solution)/shard_map/ppermute | solution.py:39
  132.7 28.5 %copy-start.32 = (bf16[256,1024]{1,0:T(8,128)(2,1)}, bf16[256,1024]{1,0:T(8,128)(2,1)S(1)}, u32[]{:S(2)}) copy-start(bf16[256,1024]{1,0:T(8,128)(2,1)S(1)} %get-tuple-element.36) | copy-start | bytes 1572868
  174.9 5.7 %collective-permute-start.21 = (bf16[512,1024]{1,0:T(8,128)(2,1)}, bf16[512,1024]{1,0:T(8,128)(2,1)S(1)}, u32[]{:S(2)}, u32[]{:S(2)}) collective-permute-start(bf16[512,1024]{1,0:T(8,128)(2,1)} %get-tuple-element.33), channel_id=1, source_target_pairs={{0,1},{1,0},{2,3},{3,2},{4,5},{5,4},{6,7},{7,6},{8,9},{9,8},{10,11... | collective-permute-start | bytes 3145736 | tf_op jit(solution)/shard_map/ppermute | solution.py:39
  174.9 16.7 %all-to-all-start.1 = ((bf16[16,48,256]{2,1,0:T(8,128)(2,1)}), bf16[16,48,256]{2,1,0:T(8,128)(2,1)S(1)}, u32[]{:S(2)}, u32[]{:S(2)}) async-start(bf16[16,48,256]{2,1,0:T(8,128)(2,1)} %copy-done.16), calls=%async_computation.1 | async-start | bytes 786432 | tf_op jit(solution)/shard_map/all_to_all | solution.py:429
  178.5 21.6 %collective-permute-start.24 = (bf16[256,1024]{1,0:T(8,128)(2,1)}, bf16[256,1024]{1,0:T(8,128)(2,1)}, u32[]{:S(2)}, u32[]{:S(2)}) collective-permute-start(bf16[256,1024]{1,0:T(8,128)(2,1)} %copy-done.33), channel_id=1, source_target_pairs={{0,2},{2,0},{4,6},{6,4},{8,10},{10,8},{12,14},{14,12},{16,18},{18,... | collective-permute-start | bytes 1572872 | tf_op jit(solution)/shard_map/ppermute | solution.py:39
  180.3 28.5 %collective-permute-start.23 = (bf16[256,1024]{1,0:T(8,128)(2,1)}, bf16[256,1024]{1,0:T(8,128)(2,1)}, u32[]{:S(2)}, u32[]{:S(2)}) collective-permute-start(bf16[256,1024]{1,0:T(8,128)(2,1)} %copy-done.32), channel_id=1, source_target_pairs={{0,2},{2,0},{4,6},{6,4},{8,10},{10,8},{12,14},{14,12},{16,18},{18,... | collective-permute-start | bytes 1572872 | tf_op jit(solution)/shard_map/ppermute | solution.py:39
  180.6 1.6 copy-start.5
  183.0 36.5 %collective-permute-start.22 = (bf16[256,1024]{1,0:T(8,128)(2,1)}, bf16[256,1024]{1,0:T(8,128)(2,1)}, u32[]{:S(2)}, u32[]{:S(2)}) collective-permute-start(bf16[256,1024]{1,0:T(8,128)(2,1)} %kv_pair.1), channel_id=1, source_target_pairs={{0,2},{2,0},{4,6},{6,4},{8,10},{10,8},{12,14},{14,12},{16,18},{18,... | collective-permute-start | bytes 1572872 | tf_op jit(solution)/shard_map/ppermute | solution.py:39
  210.6 9.0 %copy-start.6 = (f32[512,1024]{1,0:T(8,128)S(1)}, f32[512,1024]{1,0:T(8,128)}, u32[]{:S(2)}) copy-start(f32[512,1024]{1,0:T(8,128)} %copy-done.4) | copy-start | bytes 6291460
  210.6 9.0 %copy-start.22 = (bf16[2,16,1024]{2,1,0:T(8,128)(2,1)S(1)}, bf16[2,16,1024]{2,1,0:T(8,128)(2,1)}, u32[]{:S(2)}) copy-start(bf16[2,16,1024]{2,1,0:T(8,128)(2,1)} %copy-done.21) | copy-start | bytes 196612
  210.6 9.0 %copy-start.24 = (bf16[256,16]{1,0:T(8,128)(2,1)S(1)}, bf16[256,16]{1,0:T(8,128)(2,1)}, u32[]{:S(2)}) copy-start(bf16[256,16]{1,0:T(8,128)(2,1)} %copy-done.23) | copy-start | bytes 24580
  (14 other events, 12.4 us)
where the time goes:
time: 223 us; the launch traced here: 222 us
  waiting for transfers between devices  119 us (53%)
  Pallas kernels  43.7 us (20%)
  starting transfers between devices  40.1 us (18%)
  local copies, waits for them, and re-layouts  18.2 us (8%)
    ppermute x25, waiting for transfers between devices, send(): return lax.ppermute(value, axis, [(i, route(i)) for i in range(count)])  84.2 us
    all_to_all x2, waiting for transfers between devices, exchange(): lax.all_to_all(value, 'fsdp', split_axis=0, concat_axis=0, tiled=True)  34.6 us
    ppermute x25, starting transfers between devices, send(): return lax.ppermute(value, axis, [(i, route(i)) for i in range(count)])  30.4 us
    pallas_call x2, Pallas kernels, chunk_product(): pl.pallas_call(functools.partial(chunk_kernel, plan, len(arrays), kv is n...  21.4 us
    unnamed x70, local copies, waits for them, and re-layouts  17.8 us
    all_to_all x2, starting transfers between devices, exchange(): lax.all_to_all(value, 'fsdp', split_axis=0, concat_axis=0, tiled=True)  9.69 us
    pallas_call x1, Pallas kernels, paired(): pl.pallas_call(functools.partial(spread_kernel, blocks), name='spread', g...  7.78 us
  transfers between devices with their start and end apart: 27, of which 13 were waited for; matrix products, arithmetic and copies ran while one was open for 0% of the time, Pallas kernels for 13%

commit v1 on v0

--- a/solution.py
+++ b/solution.py
@@ -17,7 +17,7 @@
 ANYWHERE = pl.BlockSpec(memory_space=pl.ANY)
 VMEM = pl.BlockSpec(memory_space=pltpu.VMEM)
 SMEM = pl.BlockSpec(memory_space=pltpu.SMEM)
-LIMIT = pltpu.CompilerParams(vmem_limit_bytes=34 * 1024 * 1024)
+LIMIT = pltpu.CompilerParams(vmem_limit_bytes=28 * 1024 * 1024)
 
 ROW_ROW = (((1,), (1,)), ((), ()))
 
@@ -83,11 +83,11 @@
     take = lambda n: [refs.pop(0) for _ in range(n)]
     (place,) = take(1)
     arrays = take(array_count)
-    tok_all, tok_pair, cot_own, cot_part, cot_rest, back, down = take(7)
-    kv_in, _ = take(2) if has_kv else (None, None)
-    out, ig_pair = take(2)
+    tok_all, tok_pair, cot_own, cot_part, cot_rest = take(5)
+    (kv_in,) = take(1) if has_kv else (None,)
+    ig_own, ig_pair = take(2)
     kv_out = take(2) if last else take(1)
-    weight, tok, cot, finished, sem = refs[:5]
+    weight, tok, cot = refs[:3]
     rows = tok_all.shape[0]
     depth, total = weight.shape
     count = len(plan)
@@ -109,7 +109,7 @@
         if has_kv:
             part = part + kv_in[:, at]
         if last:
-            wide_kv, narrow_kv = refs[5:]
+            wide_kv, narrow_kv = refs[3:]
             slot = pl.ds(pl.multiple_of(lax.rem(place[i] * width, columns), LANES), width)
             where = lax.rem(lax.div(place[i] * width, columns) + core, 2)
             wide_kv[where, :, slot] = part
@@ -123,62 +123,39 @@
     cot[lower, pl.ds(pl.multiple_of(core * columns, LANES), columns)] = cot_part[...]
     cot[lower, pl.ds(pl.multiple_of((1 - core) * columns, LANES), columns)] = cot_rest[...]
     tile = min(2 * LANES, depth)
-    blocks = back.shape[0] // BLOCK
 
     @pl.loop(0, depth // tile)
     def _(step):
         at = pl.multiple_of(step * tile, tile)
-        wide = pl.ds(pl.multiple_of(base + step * tile, LANES), tile)
         part = dot(cot[...], weight[pl.ds(at, tile), :], ROW_ROW)
+        ig_own[:, pl.ds(at, tile)] = part[:rows]
         ig_pair[:, pl.ds(at, tile)] = part[rows:].astype(ig_pair.dtype)
-        for m in range(blocks):
-            own = pl.ds(m * BLOCK, BLOCK)
-            adapter = dot(back[own, :], down[m, :, wide])
-            adapter = adapter.astype(jnp.bfloat16).astype(jnp.float32)
-            both = part[m * BLOCK : (m + 1) * BLOCK] + adapter
-            finished[own, pl.ds(at, tile)] = both.astype(finished.dtype)
-
-    result = pltpu.make_async_copy(finished, out.at[:, pl.ds(base, depth)], sem)
-    result.start()
-    result.wait()
 
 
 def chunk_product(
-    place, plan, arrays, tok, tok_pair, cot, cot_part, cot_rest, back, down, kv, out, start, depth, last
+    place, plan, arrays, tok, tok_pair, cot, cot_part, cot_rest, kv, start, depth, last
 ):
     rows, half = tok_pair.shape
     total = cot.shape[1]
-    operands = [place, *arrays, tok, tok_pair, cot, cot_part, cot_rest, back, down]
-    specs = [SMEM] + [VMEM] * (len(arrays) + 7)
-    aliases = {}
+    operands = [place, *arrays, tok, tok_pair, cot, cot_part, cot_rest]
     if kv is not None:
-        aliases[len(operands) + 1] = 0
-        operands += [kv, out]
-        specs += [VMEM, ANYWHERE]
-    shapes = [
-        jax.ShapeDtypeStruct((rows, 2 * half), jnp.bfloat16),
-        jax.ShapeDtypeStruct((rows, depth), jnp.bfloat16),
-    ]
-    out_specs = [ANYWHERE, VMEM]
+        operands.append(kv)
+    shape = jax.ShapeDtypeStruct
+    shapes = [shape((rows, depth), jnp.float32), shape((rows, depth), jnp.bfloat16)]
     if last:
-        shapes.append(jax.ShapeDtypeStruct((2 * rows, total // 2), jnp.float32))
-        shapes.append(jax.ShapeDtypeStruct((2 * rows, total // 2), jnp.bfloat16))
-        out_specs += [VMEM, VMEM]
+        shapes.append(shape((2 * rows, total // 2), jnp.float32))
+        shapes.append(shape((2 * rows, total // 2), jnp.bfloat16))
     else:
-        shapes.append(jax.ShapeDtypeStruct((2 * rows, total), jnp.float32))
-        out_specs.append(VMEM)
+        shapes.append(shape((2 * rows, total), jnp.float32))
     return pl.pallas_call(
         functools.partial(chunk_kernel, plan, len(arrays), kv is not None, last, start, half),
         out_shape=tuple(shapes),
-        in_specs=specs,
-        out_specs=tuple(out_specs),
-        input_output_aliases=aliases,
+        in_specs=[SMEM] + [VMEM] * (len(operands) - 1),
+        out_specs=(VMEM,) * len(shapes),
         scratch_shapes=[
             pltpu.VMEM((depth, total), jnp.bfloat16),
             pltpu.VMEM((2 * rows, depth), jnp.bfloat16),
             pltpu.VMEM((2 * rows, total), jnp.bfloat16),
-            pltpu.VMEM((rows, depth), jnp.bfloat16),
-            pltpu.SemaphoreType.DMA,
         ]
         + [pltpu.VMEM((2, 2 * rows, total // 2), kind) for kind in (jnp.float32, jnp.bfloat16) if last],
         cost_estimate=cost(8 * rows * depth * total, 2 * depth * total + 16 * rows * total),
@@ -308,34 +285,53 @@
         out[own, :] = (base + adapter).astype(out.dtype)
 
 
-def rest_kernel(starts, half, *refs):
+def finish_kernel(starts, half, own, place, *refs):
     count = len(starts)
-    place, got, back, down, _, out = refs[0], refs[1 : 1 + count], *refs[1 + count : 5 + count]
-    finished, factors, sems = refs[5 + count :]
-    x = place[0]
-    base = pl.multiple_of((1 - x) * half, LANES)
-    load = pltpu.make_async_copy(down.at[:, :, pl.ds(base, half)], factors, sems.at[count])
-    load.start()
-    load.wait()
+    sums, (back, down), refs = refs[:count], refs[count : count + 2], refs[count + 2 :]
+    out, finished, sems = refs[-3:]
+    x = place[0] if own else 1 - place[0]
+    base = pl.multiple_of(x * half, LANES)
     copies = []
     for i, start in enumerate(starts):
-        depth = got[i].shape[1]
-        at = pl.ds(start, depth)
-        for m in range(factors.shape[0]):
-            own = pl.ds(m * BLOCK, BLOCK)
-            adapter = dot(back[own, :], factors[m, :, at]).astype(jnp.bfloat16)
-            both = got[i][own, :].astype(jnp.float32) + adapter.astype(jnp.float32)
-            finished[own, at] = both.astype(finished.dtype)
+        depth = sums[i].shape[1]
+        at = pl.ds(pl.multiple_of(base + start, LANES), depth)
+        for m in range(down.shape[0]):
+            rows = pl.ds(m * BLOCK, BLOCK)
+            adapter = dot(back[rows, :], down[m, :, at]).astype(jnp.bfloat16)
+            both = sums[i][rows, :].astype(jnp.float32) + adapter.astype(jnp.float32)
+            finished[rows, pl.ds(start, depth)] = both.astype(finished.dtype)
         copies.append(
-            pltpu.make_async_copy(
-                finished.at[:, at],
-                out.at[:, pl.ds(pl.multiple_of(base + start, LANES), depth)],
-                sems.at[i],
-            )
+            pltpu.make_async_copy(finished.at[:, pl.ds(start, depth)], out.at[:, at], sems.at[i])
         )
         copies[-1].start()
     for copy in copies:
         copy.wait()
+
+
+def finish(starts, place, sums, back, down, out):
+    rows = sums[0].shape[0]
+    half = sum(piece.shape[1] for piece in sums)
+    ranks = down.shape[1]
+    operands = [place, *sums, back, down]
+    specs = [SMEM] + [VMEM] * (len(operands) - 1)
+    aliases = {}
+    if out is not None:
+        aliases[len(operands)] = 0
+        operands.append(out)
+        specs.append(ANYWHERE)
+    return pl.pallas_call(
+        functools.partial(finish_kernel, starts, half, out is None),
+        out_shape=jax.ShapeDtypeStruct((rows, 2 * half), jnp.bfloat16),
+        in_specs=specs,
+        out_specs=ANYWHERE,
+        input_output_aliases=aliases,
+        scratch_shapes=[
+            pltpu.VMEM((rows, half), jnp.bfloat16),
+            pltpu.SemaphoreType.DMA((len(starts),)),
+        ],
+        cost_estimate=cost(2 * rows * ranks * half, 8 * rows * half),
+        compiler_params=LIMIT,
+    )(*operands)
 
 
 def paired(tokens, frozen_weight, cotangent, block_adapter_index, down_weight, up_weight):
@@ -493,8 +489,8 @@
         compiler_params=LIMIT,
     )(id_list, id_column, owned)
 
-    kv = out = None
-    got_pieces = []
+    kv = None
+    got_pieces, own_pieces = [], []
     for c, ((start, depth), own) in enumerate(zip(chunks, held)):
         arrays = [own, mine_y, theirs_y[c]]
         plan = [((0, 0, WHOLE),), ((1, start, MINE), (2, 0, THEIRS))]
@@ -515,15 +511,13 @@
             cot,
             cot_part,
             cot_rest,
-            back_rank,
-            down_mine,
             kv,
-            out,
             start,
             depth,
             last,
         )
-        out, pair = results[:2]
+        own_sum, pair = results[:2]
+        own_pieces.append(own_sum)
         kv = results[2]
         got_pieces.append(x_send(pair))
     keep, other_columns = results[2:]
@@ -548,21 +542,8 @@
         compiler_params=LIMIT,
     )(keep, core_got, pair_got, low_rank, up_mine)
     starts = tuple(start for start, _ in chunks)
-    out = pl.pallas_call(
-        functools.partial(rest_kernel, starts, half),
-        name="rest",
-        out_shape=shape((rows, shard), bf16),
-        in_specs=[SMEM] + [VMEM] * (len(starts) + 1) + [ANYWHERE, ANYWHERE],
-        out_specs=ANYWHERE,
-        input_output_aliases={len(starts) + 3: 0},
-        scratch_shapes=[
-            pltpu.VMEM((rows, half), bf16),
-            pltpu.VMEM((blocks, ranks, half), bf16),
-            pltpu.SemaphoreType.DMA((len(starts) + 1,)),
-        ],
-        cost_estimate=cost(2 * rows * ranks * half, 4 * rows * half),
-        compiler_params=LIMIT,
-    )(x.astype(jnp.int32).reshape(1), *got_pieces, back_rank, down_mine, out)
+    out = finish(starts, here, own_pieces, back_rank, down_mine, None)
+    out = finish(starts, here, got_pieces, back_rank, down_mine, out)
     return (
         key_value.reshape(batches, batch_rows, columns),
         out.reshape(batches, batch_rows, shard),

time: 223 us -> 222 us (level)
  waiting for transfers between devices: 119 us -> 94.6 us
  blocking collectives: 0 us -> 20.3 us
  local copies, waits for them, and re-layouts: 18.2 us -> 32.9 us
  starting transfers between devices: 40.1 us -> 34.1 us
  Pallas kernels: 43.7 us -> 38 us
    all_to_all x2 -> x1, waiting for transfers between devices: 34.6 us -> 6.19 us  [exchange(): lax.all_to_all(value, 'fsdp', split_axis=0, concat_axis=0, tiled=True)]
    all_to_all x0 -> x1, blocking collectives: none -> 20.3 us  [exchange(): lax.all_to_all(value, 'fsdp', split_axis=0, concat_axis=0, tiled=True)]
    unnamed x70 -> x86, local copies, waits for them, and re-layouts: 17.8 us -> 32.5 us
    all_to_all x2 -> x1, starting transfers between devices: 9.69 us -> 3.81 us  [exchange(): lax.all_to_all(value, 'fsdp', split_axis=0, concat_axis=0, tiled=True)]
    pallas_call x2, Pallas kernels: 21.4 us -> 16.9 us  [chunk_product(): pl.pallas_call(functools.partial(chunk_kernel, plan, len(arrays), kv is n...]
    ppermute x25, waiting for transfers between devices: 84.2 us -> 88.4 us  [send(): return lax.ppermute(value, axis, [(i, route(i)) for i in range(count)])]
  transfers between devices with their start and end apart: 27 -> 26, of which waited for: 13 -> 15; matrix products, arithmetic and copies ran while one was open for 0% -> 0% of each run, Pallas kernels for 13% -> 12%
where the time goes in v1:
time: 222 us; the launch traced here: 221 us
  waiting for transfers between devices  94.6 us (43%)
  Pallas kernels  38 us (17%)
  starting transfers between devices  34.1 us (15%)
  local copies, waits for them, and re-layouts  32.9 us (15%)
  blocking collectives  20.3 us (9%)
    ppermute x25, waiting for transfers between devices, send(): return lax.ppermute(value, axis, [(i, route(i)) for i in range(count)])  88.4 us
    unnamed x86, local copies, waits for them, and re-layouts  32.5 us
    ppermute x25, starting transfers between devices, send(): return lax.ppermute(value, axis, [(i, route(i)) for i in range(count)])  30.3 us
    all_to_all x1, blocking collectives, exchange(): lax.all_to_all(value, 'fsdp', split_axis=0, concat_axis=0, tiled=True)  20.3 us
    pallas_call x2, Pallas kernels, chunk_product(): pl.pallas_call(functools.partial(chunk_kernel, plan, len(arrays), kv is n...  16.9 us
    pallas_call x1, Pallas kernels, paired(): pl.pallas_call(functools.partial(spread_kernel, blocks), name='spread', g...  7.79 us
    all_to_all x1, waiting for transfers between devices, exchange(): lax.all_to_all(value, 'fsdp', split_axis=0, concat_axis=0, tiled=True)  6.19 us
  transfers between devices with their start and end apart: 26, of which 15 were waited for; matrix products, arithmetic and copies ran while one was open for 0% of the time, Pallas kernels for 12%

profile of v1, /device:TPU:0, one launch (start us, length us, event | category | flops | bytes accessed | tf_op | source)
XLA Modules:
  0.0 220.8 jit_solution(6318676522381881217)
XLA Ops:
  0.7 1.2 copy-done.7
  2.5 3.0 %collective-permute-start.12 = (bf16[1024,128]{1,0:T(8,128)(2,1)S(1)}, bf16[1024,128]{1,0:T(8,128)(2,1)S(1)}, u32[]{:S(2)}, u32[]{:S(2)}) collective-permute-start(bf16[1024,128]{1,0:T(8,128)(2,1)S(1)} %first.1), channel_id=1, source_target_pairs={{0,2},{2,0},{4,6},{6,4},{8,10},{10,8},{12,14},{14,12},{16,18},{18,... | collective-permute-start | bytes 786440 | tf_op jit(solution)/shard_map/ppermute | solution.py:39
  5.6 1.6 copy-done
  9.2 2.7 %collective-permute-done.12.theirs = bf16[1024,128]{1,0:T(8,128)(2,1)S(1)} collective-permute-done((bf16[1024,128]{1,0:T(8,128)(2,1)S(1)}, bf16[1024,128]{1,0:T(8,128)(2,1)S(1)}, u32[]{:S(2)}, u32[]{:S(2)}) %collective-permute-start.12) | collective-permute-done | bytes 262176 | tf_op jit(solution)/shard_map/ppermute | solution.py:39
  12.5 1.9 collective-permute-start.14
  14.4 1.5 collective-permute-start
  15.9 5.4 %collective-permute-done.theirs = bf16[1024,128]{1,0:T(8,128)(2,1)S(1)} collective-permute-done((bf16[1024,128]{1,0:T(8,128)(2,1)S(1)}, bf16[1024,128]{1,0:T(8,128)(2,1)S(1)}, u32[]{:S(2)}, u32[]{:S(2)}) %collective-permute-start) | collective-permute-done | bytes 262176 | tf_op jit(solution)/shard_map/ppermute | solution.py:39
  22.0 1.6 collective-permute-start.3
  24.4 1.5 collective-permute-start.10
  25.9 3.3 %collective-permute-done.14.refs_4_ = bf16[1024,256]{1,0:T(8,128)(2,1)S(1)} collective-permute-done((bf16[1024,256]{1,0:T(8,128)(2,1)S(1)}, bf16[1024,256]{1,0:T(8,128)(2,1)S(1)}, u32[]{:S(2)}, u32[]{:S(2)}) %collective-permute-start.14) | collective-permute-done | bytes 524320 | tf_op jit(solution)/shard_map/ppermute | solution.py:39
  29.2 1.7 collective-permute-start.1
  30.9 1.5 collective-permute-start.9
  32.4 8.1 %collective-permute-done.3.refs_4_ = bf16[1024,256]{1,0:T(8,128)(2,1)} collective-permute-done((bf16[1024,256]{1,0:T(8,128)(2,1)S(1)}, bf16[1024,256]{1,0:T(8,128)(2,1)}, u32[]{:S(2)}, u32[]{:S(2)}) %collective-permute-start.3) | collective-permute-done | bytes 524320 | tf_op jit(solution)/shard_map/ppermute | solution.py:39
  41.4 10.4 %collective-permute-done.16.refs_6_ = bf16[1024,256]{1,0:T(8,128)(2,1)} collective-permute-done((bf16[1024,256]{1,0:T(8,128)(2,1)S(1)}, bf16[1024,256]{1,0:T(8,128)(2,1)}, u32[]{:S(2)}, u32[]{:S(2)}) %collective-permute-start.16) | collective-permute-done | bytes 524320 | tf_op jit(solution)/shard_map/ppermute | solution.py:39
  52.6 1.7 collective-permute-start.13
  54.3 5.4 %collective-permute-done.13.refs_3_ = bf16[1024,128]{1,0:T(8,128)(2,1)S(1)} collective-permute-done((bf16[1024,128]{1,0:T(8,128)(2,1)S(1)}, bf16[1024,128]{1,0:T(8,128)(2,1)S(1)}, u32[]{:S(2)}, u32[]{:S(2)}) %collective-permute-start.13) | collective-permute-done | bytes 262176 | tf_op jit(solution)/shard_map/ppermute | solution.py:39
  60.4 2.2 collective-permute-start.15
  63.4 1.7 collective-permute-start.7
  66.4 7.8 %collective-permute-done.18.refs_8_ = bf16[1024,256]{1,0:T(8,128)(2,1)} collective-permute-done((bf16[1024,256]{1,0:T(8,128)(2,1)}, bf16[1024,256]{1,0:T(8,128)(2,1)}, u32[]{:S(2)}, u32[]{:S(2)}) %collective-permute-start.18) | collective-permute-done | bytes 524320 | tf_op jit(solution)/shard_map/ppermute | solution.py:39
  74.2 1.7 collective-permute-start.19
  78.1 1.7 collective-permute-start.6
  79.8 3.9 %collective-permute-done.7.refs_8_ = bf16[1024,256]{1,0:T(8,128)(2,1)} collective-permute-done((bf16[1024,256]{1,0:T(8,128)(2,1)}, bf16[1024,256]{1,0:T(8,128)(2,1)}, u32[]{:S(2)}, u32[]{:S(2)}) %collective-permute-start.7) | collective-permute-done | bytes 524320 | tf_op jit(solution)/shard_map/ppermute | solution.py:39
  83.8 1.5 collective-permute-start.8
  85.4 1.3 collective-permute-done.17.refs_7_
  86.7 2.0 collective-permute-start.2
  88.7 9.2 %collective-permute-done.19.refs_9_ = bf16[1024,256]{1,0:T(8,128)(2,1)} collective-permute-done((bf16[1024,256]{1,0:T(8,128)(2,1)}, bf16[1024,256]{1,0:T(8,128)(2,1)}, u32[]{:S(2)}, u32[]{:S(2)}) %collective-permute-start.19) | collective-permute-done | bytes 524320 | tf_op jit(solution)/shard_map/ppermute | solution.py:39
  99.0 1.2 copy-done.26
  106.4 8.0 %shard_map.95 = (f32[256,1024]{1,0:T(8,128)S(1)}, bf16[256,1024]{1,0:T(8,128)(2,1)S(1)}, f32[512,2048]{1,0:T(8,128)S(1)}) custom-call(s32[10]{0:T(128)S(1)} %stack.59.refs_0_, bf16[1024,256]{1,0:T(8,128)(2,1)S(1)} %copy-done.17, bf16[2048,128]{1,0:T(8,128)(2,1)S(1)} %copy-done.33, bf16[1024,128]{1,0:T(8,128)(2,1)S(1)} %copy-done.41, ...), custom_call_target="tpu_custom_call" | custom-call | flops 4294967296 | bytes 12582912 | tf_op jit(solution)/shard_map/pallas_call | solution.py:150
  115.3 16.7 %collective-permute-done.2.refs_3_ = bf16[1024,128]{1,0:T(8,128)(2,1)S(1)} collective-permute-done((bf16[1024,128]{1,0:T(8,128)(2,1)S(1)}, bf16[1024,128]{1,0:T(8,128)(2,1)S(1)}, u32[]{:S(2)}, u32[]{:S(2)}) %collective-permute-start.2) | collective-permute-done | bytes 262176 | tf_op jit(solution)/shard_map/ppermute | solution.py:39
  132.0 8.9 %shard_map.96 = (f32[256,1024]{1,0:T(8,128)S(1)}, bf16[256,1024]{1,0:T(8,128)(2,1)S(1)}, f32[512,1024]{1,0:T(8,128)S(1)}, bf16[512,1024]{1,0:T(8,128)(2,1)}) custom-call(s32[10]{0:T(128)S(1)} %stack.59.refs_0_, bf16[1024,256]{1,0:T(8,128)(2,1)S(1)} %copy-done.15, bf16[2048,128]{1,0:T(8,128)(2,1)S(1)} %copy-done.33, ...), custom_call_target="tpu_custom_call" | custom-call | flops 4294967296 | bytes 12582912 | tf_op jit(solution)/shard_map/pallas_call | solution.py:150
  140.9 1.3 copy-done.4
  144.3 2.2 copy-done.8
  147.7 2.1 fetch.1
  149.9 20.3 %all_to_all.10.got = bf16[16,48,256]{2,1,0:T(8,128)(2,1)S(1)} all-to-all(bf16[16,48,256]{2,1,0:T(8,128)(2,1)S(1)} %fetch.1), channel_id=1, replica_groups=mesh['fsdp'=16,'tp'=2] {'fsdp'}, dimensions={0} | all-to-all | bytes 786432 | tf_op jit(solution)/shard_map/all_to_all | solution.py:425
  170.9 1.2 collective-permute-done.22.other
  174.1 3.8 %all-to-all-start.1 = ((bf16[16,48,256]{2,1,0:T(8,128)(2,1)}), bf16[16,48,256]{2,1,0:T(8,128)(2,1)S(1)}, u32[]{:S(2)}, u32[]{:S(2)}) async-start(bf16[16,48,256]{2,1,0:T(8,128)(2,1)} %copy-done.18), calls=%async_computation.1 | async-start | bytes 786432 | tf_op jit(solution)/shard_map/all_to_all | solution.py:425
  177.9 1.9 collective-permute-start.24
  180.0 1.6 copy-done.5
  181.6 1.3 kv_pair.1
  182.9 1.9 collective-permute-start.21
  184.8 6.2 %all-to-all-done.1.got = bf16[16,48,256]{2,1,0:T(8,128)(2,1)S(1)} async-done(((bf16[16,48,256]{2,1,0:T(8,128)(2,1)}), bf16[16,48,256]{2,1,0:T(8,128)(2,1)S(1)}, u32[]{:S(2)}, u32[]{:S(2)}) %all-to-all-start.1) | async-done | bytes 393248 | tf_op jit(solution)/shard_map/all_to_all | solution.py:425
  191.0 7.8 %spread.1 = (f32[512,16,256]{2,1,0:T(8,128)}, f32[1024,512]{1,0:T(8,128)}) custom-call(s32[32]{0:T(128)S(1)} %copy-done.24, s32[32,1]{1,0:T(8,128)S(1)} %reshape.42.ids_column, bf16[16,48,256]{2,1,0:T(8,128)(2,1)S(1)} %all-to-all-done.1.got), custom_call_target="tpu_custom_call" | custom-call | bytes 10485760 | tf_op jit(solution)/shard_map/spread/pallas_call | solution.py:474
  198.8 1.2 copy-done.10
  201.9 1.8 shard_map.97.refs_4_
  203.8 4.5 %collective-permute-done.23.refs_0_ = bf16[256,1024]{1,0:T(8,128)(2,1)S(1)} collective-permute-done((bf16[256,1024]{1,0:T(8,128)(2,1)}, bf16[256,1024]{1,0:T(8,128)(2,1)S(1)}, u32[]{:S(2)}, u32[]{:S(2)}) %collective-permute-start.23) | collective-permute-done | bytes 524320 | tf_op jit(solution)/shard_map/ppermute | solution.py:39
  208.2 1.8 shard_map.98
  210.1 8.4 %collective-permute-done.21.pair_got = bf16[256,1024]{1,0:T(8,128)(2,1)S(1)} collective-permute-done((bf16[256,1024]{1,0:T(8,128)(2,1)S(1)}, bf16[256,1024]{1,0:T(8,128)(2,1)S(1)}, u32[]{:S(2)}, u32[]{:S(2)}) %collective-permute-start.21) | collective-permute-done | bytes 524320 | tf_op jit(solution)/shard_map/ppermute | solution.py:39
  218.4 2.4 %kv_end.1 = bf16[256,1024]{1,0:T(8,128)(2,1)} custom-call(f32[512,1024]{1,0:T(8,128)S(1)} %copy-done.6, bf16[512,1024]{1,0:T(8,128)(2,1)} %collective-permute-done.20.got.core_got, bf16[256,1024]{1,0:T(8,128)(2,1)S(1)} %collective-permute-done.21.pair_got, bf16[256,16]{1,0:T(8,128)(2,1)S(1)} %copy-done.20, bf16[2,16,1024]{2,1,0:T(8,128)(2,1)S(1)} %get-tuple-element.32.up), custom_call_target="tpu_custom_call" | custom-call | flops 8388608 | bytes 3145728 | tf_op jit(solution)/shard_map/kv_end/pallas_call | solution.py:535
  (110 shorter events, 27.5 us)
Async XLA Ops:
  0.7 1.2 copy-start.7
  1.9 19.4 %copy-start.21 = (s32[2]{0:T(128)}, s32[2]{0:T(128)S(1)}, u32[]{:S(2)}) copy-start(s32[2]{0:T(128)S(1)} %pad_add_fusion.place) | copy-start | bytes 28
  2.5 9.3 %collective-permute-start.12 = (bf16[1024,128]{1,0:T(8,128)(2,1)S(1)}, bf16[1024,128]{1,0:T(8,128)(2,1)S(1)}, u32[]{:S(2)}, u32[]{:S(2)}) collective-permute-start(bf16[1024,128]{1,0:T(8,128)(2,1)S(1)} %first.1), channel_id=1, source_target_pairs={{0,2},{2,0},{4,6},{6,4},{8,10},{10,8},{12,14},{14,12},{16,18},{18,... | collective-permute-start | bytes 786440 | tf_op jit(solution)/shard_map/ppermute | solution.py:39
  5.6 1.6 copy-start
  7.2 1.2 copy-start.2
  8.4 89.6 %copy-start.3 = (bf16[2,128,2048]{2,1,0:T(8,128)(2,1)S(1)}, bf16[2,128,2048]{2,1,0:T(8,128)(2,1)}, u32[]{:S(2)}) copy-start(bf16[2,128,2048]{2,1,0:T(8,128)(2,1)} %param.8) | copy-start | bytes 3145732
  9.1 88.8 %copy-start.1 = (bf16[2,128,4096]{2,1,0:T(8,128)(2,1)S(1)}, bf16[2,128,4096]{2,1,0:T(8,128)(2,1)}, u32[]{:S(2)}) copy-start(bf16[2,128,4096]{2,1,0:T(8,128)(2,1)} %param.6) | copy-start | bytes 6291460
  12.5 39.3 %copy-start.16 = (bf16[1024,256]{1,0:T(8,128)(2,1)}, bf16[1024,256]{1,0:T(8,128)(2,1)S(1)}, u32[]{:S(2)}) copy-start(bf16[1024,256]{1,0:T(8,128)(2,1)S(1)} %shard_map.94.refs_1_) | copy-start | bytes 1572868
  12.5 16.7 %collective-permute-start.14 = (bf16[1024,256]{1,0:T(8,128)(2,1)S(1)}, bf16[1024,256]{1,0:T(8,128)(2,1)S(1)}, u32[]{:S(2)}, u32[]{:S(2)}) collective-permute-start(bf16[1024,256]{1,0:T(8,128)(2,1)S(1)} %shard_map.94.refs_1_), channel_id=1, source_target_pairs={{0,8},{2,10},{4,12},{6,14},{8,16},{10,18},{12,20},{14,22},{16,24},... | collective-permute-start | bytes 1572872 | tf_op jit(solution)/shard_map/ppermute | solution.py:39
  14.4 6.9 %collective-permute-start = (bf16[1024,128]{1,0:T(8,128)(2,1)S(1)}, bf16[1024,128]{1,0:T(8,128)(2,1)S(1)}, u32[]{:S(2)}, u32[]{:S(2)}) collective-permute-start(bf16[1024,128]{1,0:T(8,128)(2,1)S(1)} %get-tuple-element.24), channel_id=1, source_target_pairs={{0,2},{2,0},{4,6},{6,4},{8,10},{10,8},{12,14},{14,12},{16,18},{18,... | collective-permute-start | bytes 786440 | tf_op jit(solution)/shard_map/ppermute | solution.py:39
  22.0 18.6 %collective-permute-start.3 = (bf16[1024,256]{1,0:T(8,128)(2,1)S(1)}, bf16[1024,256]{1,0:T(8,128)(2,1)}, u32[]{:S(2)}, u32[]{:S(2)}) collective-permute-start(bf16[1024,256]{1,0:T(8,128)(2,1)S(1)} %shard_map.93.refs_1_), channel_id=1, source_target_pairs={{0,8},{2,10},{4,12},{6,14},{8,16},{10,18},{12,20},{14,22},{16,24},... | collective-permute-start | bytes 1572872 | tf_op jit(solution)/shard_map/ppermute | solution.py:39
  24.4 16.2 %collective-permute-start.10 = (bf16[256,1024]{1,0:T(8,128)(2,1)S(1)}, bf16[256,1024]{1,0:T(8,128)(2,1)S(1)}, u32[]{:S(2)}, u32[]{:S(2)}) collective-permute-start(bf16[256,1024]{1,0:T(8,128)(2,1)S(1)} %get-tuple-element.26), channel_id=1, source_target_pairs={{0,2},{2,0},{4,6},{6,4},{8,10},{10,8},{12,14},{14,12},{16,18},{18,... | collective-permute-start | bytes 1572872 | tf_op jit(solution)/shard_map/ppermute | solution.py:39
  29.2 22.6 %collective-permute-start.16 = (bf16[1024,256]{1,0:T(8,128)(2,1)S(1)}, bf16[1024,256]{1,0:T(8,128)(2,1)}, u32[]{:S(2)}, u32[]{:S(2)}) collective-permute-start(bf16[1024,256]{1,0:T(8,128)(2,1)S(1)} %collective-permute-done.14.refs_4_), channel_id=1, source_target_pairs={{0,8},{2,10},{4,12},{6,14},{8,16},{10,18},{12,20},{14,22},{16,24},... | collective-permute-start | bytes 1572872 | tf_op jit(solution)/shard_map/ppermute | solution.py:39
  29.2 22.6 %collective-permute-start.1 = (bf16[2048,128]{1,0:T(8,128)(2,1)S(1)}, bf16[2048,128]{1,0:T(8,128)(2,1)S(1)}, u32[]{:S(2)}, u32[]{:S(2)}) collective-permute-start(bf16[2048,128]{1,0:T(8,128)(2,1)S(1)} %get-tuple-element.23.mine), channel_id=1, source_target_pairs={{0,4},{2,6},{4,0},{6,2},{8,12},{10,14},{12,8},{14,10},{16,20},{18,... | collective-permute-start | bytes 1572872 | tf_op jit(solution)/shard_map/ppermute | solution.py:39
  30.9 45.0 %collective-permute-start.9 = (bf16[256,2048]{1,0:T(8,128)(2,1)S(1)}, bf16[256,2048]{1,0:T(8,128)(2,1)S(1)}, u32[]{:S(2)}, u32[]{:S(2)}) collective-permute-start(bf16[256,2048]{1,0:T(8,128)(2,1)S(1)} %get-tuple-element.25), channel_id=1, source_target_pairs={{0,2},{2,0},{4,6},{6,4},{8,10},{10,8},{12,14},{14,12},{16,18},{18,... | collective-permute-start | bytes 3145736 | tf_op jit(solution)/shard_map/ppermute | solution.py:39
  40.5 22.9 %collective-permute-start.5 = (bf16[1024,256]{1,0:T(8,128)(2,1)}, bf16[1024,256]{1,0:T(8,128)(2,1)}, u32[]{:S(2)}, u32[]{:S(2)}) collective-permute-start(bf16[1024,256]{1,0:T(8,128)(2,1)} %collective-permute-done.3.refs_4_), channel_id=1, source_target_pairs={{0,8},{2,10},{4,12},{6,14},{8,16},{10,18},{12,20},{14,22},{16,24},... | collective-permute-start | bytes 1572872 | tf_op jit(solution)/shard_map/ppermute | solution.py:39
  40.5 24.6 %collective-permute-start.11 = (bf16[256,1024]{1,0:T(8,128)(2,1)S(1)}, bf16[256,1024]{1,0:T(8,128)(2,1)S(1)}, u32[]{:S(2)}, u32[]{:S(2)}) collective-permute-start(bf16[256,1024]{1,0:T(8,128)(2,1)S(1)} %collective-permute-done.10.refs_13_), channel_id=1, source_target_pairs={{0,1},{1,0},{2,3},{3,2},{4,5},{5,4},{6,7},{7,6},{8,9},{9,8},{10,11... | collective-permute-start | bytes 1572872 | tf_op jit(solution)/shard_map/ppermute | solution.py:39
  51.8 22.5 %collective-permute-start.18 = (bf16[1024,256]{1,0:T(8,128)(2,1)}, bf16[1024,256]{1,0:T(8,128)(2,1)}, u32[]{:S(2)}, u32[]{:S(2)}) collective-permute-start(bf16[1024,256]{1,0:T(8,128)(2,1)} %collective-permute-done.16.refs_6_), channel_id=1, source_target_pairs={{0,8},{2,10},{4,12},{6,14},{8,16},{10,18},{12,20},{14,22},{16,24},... | collective-permute-start | bytes 1572872 | tf_op jit(solution)/shard_map/ppermute | solution.py:39
  52.6 7.1 %collective-permute-start.13 = (bf16[1024,128]{1,0:T(8,128)(2,1)S(1)}, bf16[1024,128]{1,0:T(8,128)(2,1)S(1)}, u32[]{:S(2)}, u32[]{:S(2)}) collective-permute-start(bf16[1024,128]{1,0:T(8,128)(2,1)S(1)} %collective-permute-done.12.theirs), channel_id=1, source_target_pairs={{0,4},{2,6},{4,0},{6,2},{8,12},{10,14},{12,8},{14,10},{16,20},{18,... | collective-permute-start | bytes 786440 | tf_op jit(solution)/shard_map/ppermute | solution.py:39
  60.4 16.8 %collective-permute-start.15 = (bf16[1024,256]{1,0:T(8,128)(2,1)S(1)}, bf16[1024,256]{1,0:T(8,128)(2,1)S(1)}, u32[]{:S(2)}, u32[]{:S(2)}) collective-permute-start(bf16[1024,256]{1,0:T(8,128)(2,1)S(1)} %collective-permute-done.14.refs_4_), channel_id=1, source_target_pairs={{0,4},{2,6},{4,0},{6,2},{8,12},{10,14},{12,8},{14,10},{16,20},{18,... | collective-permute-start | bytes 1572872 | tf_op jit(solution)/shard_map/ppermute | solution.py:39
  63.4 20.4 %collective-permute-start.7 = (bf16[1024,256]{1,0:T(8,128)(2,1)}, bf16[1024,256]{1,0:T(8,128)(2,1)}, u32[]{:S(2)}, u32[]{:S(2)}) collective-permute-start(bf16[1024,256]{1,0:T(8,128)(2,1)} %collective-permute-done.5.refs_6_), channel_id=1, source_target_pairs={{0,8},{2,10},{4,12},{6,14},{8,16},{10,18},{12,20},{14,22},{16,24},... | collective-permute-start | bytes 1572872 | tf_op jit(solution)/shard_map/ppermute | solution.py:39
  65.9 20.8 %collective-permute-start.17 = (bf16[1024,256]{1,0:T(8,128)(2,1)}, bf16[1024,256]{1,0:T(8,128)(2,1)}, u32[]{:S(2)}, u32[]{:S(2)}) collective-permute-start(bf16[1024,256]{1,0:T(8,128)(2,1)} %collective-permute-done.16.refs_6_), channel_id=1, source_target_pairs={{0,4},{2,6},{4,0},{6,2},{8,12},{10,14},{12,8},{14,10},{16,20},{18,... | collective-permute-start | bytes 1572872 | tf_op jit(solution)/shard_map/ppermute | solution.py:39
  74.2 23.7 %collective-permute-start.19 = (bf16[1024,256]{1,0:T(8,128)(2,1)}, bf16[1024,256]{1,0:T(8,128)(2,1)}, u32[]{:S(2)}, u32[]{:S(2)}) collective-permute-start(bf16[1024,256]{1,0:T(8,128)(2,1)} %collective-permute-done.18.refs_8_), channel_id=1, source_target_pairs={{0,4},{2,6},{4,0},{6,2},{8,12},{10,14},{12,8},{14,10},{16,20},{18,... | collective-permute-start | bytes 1572872 | tf_op jit(solution)/shard_map/ppermute | solution.py:39
  77.0 55.0 %collective-permute-start.4 = (bf16[1024,256]{1,0:T(8,128)(2,1)}, bf16[1024,256]{1,0:T(8,128)(2,1)}, u32[]{:S(2)}, u32[]{:S(2)}) collective-permute-start(bf16[1024,256]{1,0:T(8,128)(2,1)} %collective-permute-done.3.refs_4_), channel_id=1, source_target_pairs={{0,4},{2,6},{4,0},{6,2},{8,12},{10,14},{12,8},{14,10},{16,20},{18,... | collective-permute-start | bytes 1572872 | tf_op jit(solution)/shard_map/ppermute | solution.py:39
  78.1 53.9 %collective-permute-start.6 = (bf16[1024,256]{1,0:T(8,128)(2,1)}, bf16[1024,256]{1,0:T(8,128)(2,1)}, u32[]{:S(2)}, u32[]{:S(2)}) collective-permute-start(bf16[1024,256]{1,0:T(8,128)(2,1)} %collective-permute-done.5.refs_6_), channel_id=1, source_target_pairs={{0,4},{2,6},{4,0},{6,2},{8,12},{10,14},{12,8},{14,10},{16,20},{18,... | collective-permute-start | bytes 1572872 | tf_op jit(solution)/shard_map/ppermute | solution.py:39
  83.8 48.2 %collective-permute-start.8 = (bf16[1024,256]{1,0:T(8,128)(2,1)}, bf16[1024,256]{1,0:T(8,128)(2,1)}, u32[]{:S(2)}, u32[]{:S(2)}) collective-permute-start(bf16[1024,256]{1,0:T(8,128)(2,1)} %collective-permute-done.7.refs_8_), channel_id=1, source_target_pairs={{0,4},{2,6},{4,0},{6,2},{8,12},{10,14},{12,8},{14,10},{16,20},{18,... | collective-permute-start | bytes 1572872 | tf_op jit(solution)/shard_map/ppermute | solution.py:39
  85.4 46.6 %copy-start.15 = (bf16[1024,256]{1,0:T(8,128)(2,1)S(1)}, bf16[1024,256]{1,0:T(8,128)(2,1)}, u32[]{:S(2)}) copy-start(bf16[1024,256]{1,0:T(8,128)(2,1)} %copy-done.14) | copy-start | bytes 1572868
  86.7 45.3 %collective-permute-start.2 = (bf16[1024,128]{1,0:T(8,128)(2,1)S(1)}, bf16[1024,128]{1,0:T(8,128)(2,1)S(1)}, u32[]{:S(2)}, u32[]{:S(2)}) collective-permute-start(bf16[1024,128]{1,0:T(8,128)(2,1)S(1)} %collective-permute-done.theirs), channel_id=1, source_target_pairs={{0,4},{2,6},{4,0},{6,2},{8,12},{10,14},{12,8},{14,10},{16,20},{18,... | collective-permute-start | bytes 786440 | tf_op jit(solution)/shard_map/ppermute | solution.py:39
  99.0 1.2 copy-start.26
  106.4 25.6 %copy-start.27 = (bf16[256,2048]{1,0:T(8,128)(2,1)S(1)}, bf16[256,2048]{1,0:T(8,128)(2,1)}, u32[]{:S(2)}) copy-start(bf16[256,2048]{1,0:T(8,128)(2,1)} %copy-done.25) | copy-start | bytes 3145732
  115.3 16.7 %copy-start.38 = (bf16[256,1024]{1,0:T(8,128)(2,1)}, bf16[256,1024]{1,0:T(8,128)(2,1)S(1)}, u32[]{:S(2)}) copy-start(bf16[256,1024]{1,0:T(8,128)(2,1)S(1)} %get-tuple-element.33) | copy-start | bytes 1572868
  132.0 12.0 %copy-start.42 = (s32[2,16]{1,0:T(2,128)S(1)}, s32[2,16]{1,0:T(2,128)}, u32[]{:S(2)}) copy-start(s32[2,16]{1,0:T(2,128)} %param.9) | copy-start | bytes 388
  140.9 1.3 copy-start.4
  144.0 36.0 %collective-permute-start.20 = (bf16[512,1024]{1,0:T(8,128)(2,1)}, bf16[512,1024]{1,0:T(8,128)(2,1)}, u32[]{:S(2)}, u32[]{:S(2)}) collective-permute-start(bf16[512,1024]{1,0:T(8,128)(2,1)} %get-tuple-element.29), channel_id=1, source_target_pairs={{0,1},{1,0},{2,3},{3,2},{4,5},{5,4},{6,7},{7,6},{8,9},{9,8},{10,11... | collective-permute-start | bytes 3145736 | tf_op jit(solution)/shard_map/ppermute | solution.py:39
  144.3 5.6 %copy-start.23 = (s32[32]{0:T(128)}, s32[32]{0:T(128)S(1)}, u32[]{:S(2)}) copy-start(s32[32]{0:T(128)S(1)} %reshape_reshape.3.ids) | copy-start | bytes 388
  144.3 2.2 copy-start.8
  146.5 1.2 copy-start.13
  170.9 1.2 collective-permute-start.22
  174.1 16.9 %copy-start.24 = (s32[32]{0:T(128)S(1)}, s32[32]{0:T(128)}, u32[]{:S(2)}) copy-start(s32[32]{0:T(128)} %copy-done.23) | copy-start | bytes 388
  174.1 16.9 %all-to-all-start.1 = ((bf16[16,48,256]{2,1,0:T(8,128)(2,1)}), bf16[16,48,256]{2,1,0:T(8,128)(2,1)S(1)}, u32[]{:S(2)}, u32[]{:S(2)}) async-start(bf16[16,48,256]{2,1,0:T(8,128)(2,1)} %copy-done.18), calls=%async_computation.1 | async-start | bytes 786432 | tf_op jit(solution)/shard_map/all_to_all | solution.py:425
  177.9 25.9 %collective-permute-start.24 = (bf16[256,1024]{1,0:T(8,128)(2,1)}, bf16[256,1024]{1,0:T(8,128)(2,1)S(1)}, u32[]{:S(2)}, u32[]{:S(2)}) collective-permute-start(bf16[256,1024]{1,0:T(8,128)(2,1)} %copy-done.39), channel_id=1, source_target_pairs={{0,2},{2,0},{4,6},{6,4},{8,10},{10,8},{12,14},{14,12},{16,18},{18,... | collective-permute-start | bytes 1572872 | tf_op jit(solution)/shard_map/ppermute | solution.py:39
  179.8 28.4 %collective-permute-start.23 = (bf16[256,1024]{1,0:T(8,128)(2,1)}, bf16[256,1024]{1,0:T(8,128)(2,1)S(1)}, u32[]{:S(2)}, u32[]{:S(2)}) collective-permute-start(bf16[256,1024]{1,0:T(8,128)(2,1)} %copy-done.38), channel_id=1, source_target_pairs={{0,2},{2,0},{4,6},{6,4},{8,10},{10,8},{12,14},{14,12},{16,18},{18,... | collective-permute-start | bytes 1572872 | tf_op jit(solution)/shard_map/ppermute | solution.py:39
  180.0 1.6 copy-start.5
  182.9 35.5 %collective-permute-start.21 = (bf16[256,1024]{1,0:T(8,128)(2,1)S(1)}, bf16[256,1024]{1,0:T(8,128)(2,1)S(1)}, u32[]{:S(2)}, u32[]{:S(2)}) collective-permute-start(bf16[256,1024]{1,0:T(8,128)(2,1)S(1)} %kv_pair.1), channel_id=1, source_target_pairs={{0,2},{2,0},{4,6},{6,4},{8,10},{10,8},{12,14},{14,12},{16,18},{18,... | collective-permute-start | bytes 1572872 | tf_op jit(solution)/shard_map/ppermute | solution.py:39
  198.8 1.2 copy-start.10
  200.0 1.2 copy-start.12
  203.7 14.7 %copy-start.6 = (f32[512,1024]{1,0:T(8,128)S(1)}, f32[512,1024]{1,0:T(8,128)}, u32[]{:S(2)}) copy-start(f32[512,1024]{1,0:T(8,128)} %copy-done.4) | copy-start | bytes 6291460
  203.7 14.7 %copy-start.20 = (bf16[256,16]{1,0:T(8,128)(2,1)S(1)}, bf16[256,16]{1,0:T(8,128)(2,1)}, u32[]{:S(2)}) copy-start(bf16[256,16]{1,0:T(8,128)(2,1)} %copy-done.19) | copy-start | bytes 24580
  (21 other events, 18.5 us)

commit v2 on v1

--- a/solution.py
+++ b/solution.py
@@ -78,15 +78,16 @@
 WHOLE, MINE, THEIRS = 0, 1, 2
 
 
-def chunk_kernel(plan, array_count, has_kv, last, start, half, *refs):
+def chunk_kernel(plan, array_count, modes, has_kv, last, start, half, *refs):
     refs = list(refs)
     take = lambda n: [refs.pop(0) for _ in range(n)]
     (place,) = take(1)
     arrays = take(array_count)
     tok_all, tok_pair, cot_own, cot_part, cot_rest = take(5)
     (kv_in,) = take(1) if has_kv else (None,)
-    ig_own, ig_pair = take(2)
-    kv_out = take(2) if last else take(1)
+    forward, backward = "kv" in modes, "ig" in modes
+    ig_own, ig_pair = take(2) if backward else (None, None)
+    kv_out = take(1 + last) if forward else None
     weight, tok, cot = refs[:3]
     rows = tok_all.shape[0]
     depth, total = weight.shape
@@ -96,8 +97,9 @@
     x, core = place[count], place[count + 1]
     base = pl.multiple_of(x * half + start, LANES)
     lower = pl.ds(rows, rows)
-    tok[pl.ds(0, rows), :] = tok_all[:, pl.ds(base, depth)]
-    tok[lower, :] = tok_pair[:, pl.ds(start, depth)]
+    if forward:
+        tok[pl.ds(0, rows), :] = tok_all[:, pl.ds(base, depth)]
+        tok[lower, :] = tok_pair[:, pl.ds(start, depth)]
     for i, pieces in enumerate(plan):
         for array, offset, kind in pieces:
             wide = arrays[array].shape[1]
@@ -105,6 +107,8 @@
             target = pl.ds(pl.multiple_of(place[i] * width + shift, LANES), wide)
             weight[:, target] = arrays[array][pl.ds(offset, depth), :]
         at = pl.ds(pl.multiple_of(place[i] * width, LANES), width)
+        if not forward:
+            continue
         part = dot(tok[...], weight[:, at])
         if has_kv:
             part = part + kv_in[:, at]
@@ -116,9 +120,11 @@
             narrow_kv[where, :, slot] = part.astype(narrow_kv.dtype)
         else:
             kv_out[0][:, at] = part
-    if last:
+    if last and forward:
         kv_out[0][...] = wide_kv[0]
         kv_out[1][...] = narrow_kv[1]
+    if not backward:
+        return
     cot[pl.ds(0, rows), :] = cot_own[...]
     cot[lower, pl.ds(pl.multiple_of(core * columns, LANES), columns)] = cot_part[...]
     cot[lower, pl.ds(pl.multiple_of((1 - core) * columns, LANES), columns)] = cot_rest[...]
@@ -133,7 +139,7 @@
 
 
 def chunk_product(
-    place, plan, arrays, tok, tok_pair, cot, cot_part, cot_rest, kv, start, depth, last
+    place, plan, arrays, tok, tok_pair, cot, cot_part, cot_rest, kv, start, depth, last, modes
 ):
     rows, half = tok_pair.shape
     total = cot.shape[1]
@@ -141,14 +147,18 @@
     if kv is not None:
         operands.append(kv)
     shape = jax.ShapeDtypeStruct
-    shapes = [shape((rows, depth), jnp.float32), shape((rows, depth), jnp.bfloat16)]
-    if last:
+    shapes = []
+    if "ig" in modes:
+        shapes += [shape((rows, depth), jnp.float32), shape((rows, depth), jnp.bfloat16)]
+    if "kv" not in modes:
+        pass
+    elif last:
         shapes.append(shape((2 * rows, total // 2), jnp.float32))
         shapes.append(shape((2 * rows, total // 2), jnp.bfloat16))
     else:
         shapes.append(shape((2 * rows, total), jnp.float32))
     return pl.pallas_call(
-        functools.partial(chunk_kernel, plan, len(arrays), kv is not None, last, start, half),
+        functools.partial(chunk_kernel, plan, len(arrays), modes, kv is not None, last, start, half),
         out_shape=tuple(shapes),
         in_specs=[SMEM] + [VMEM] * (len(operands) - 1),
         out_specs=(VMEM,) * len(shapes),
@@ -157,8 +167,8 @@
             pltpu.VMEM((2 * rows, depth), jnp.bfloat16),
             pltpu.VMEM((2 * rows, total), jnp.bfloat16),
         ]
-        + [pltpu.VMEM((2, 2 * rows, total // 2), kind) for kind in (jnp.float32, jnp.bfloat16) if last],
-        cost_estimate=cost(8 * rows * depth * total, 2 * depth * total + 16 * rows * total),
+        + [pltpu.VMEM((2, 2 * rows, total // 2), kind) for kind in (jnp.float32, jnp.bfloat16) if last and "kv" in modes],
+        cost_estimate=cost(4 * len(modes) * rows * depth * total, 2 * depth * total + 16 * rows * total),
         compiler_params=LIMIT,
     )(*operands)
 
@@ -502,25 +512,22 @@
             plan += [((len(arrays), 0, WHOLE),), ((len(arrays) + 1, 0, WHOLE),)]
             arrays += [own, y_send(own)]
         last = start + depth == half
-        results = chunk_product(
-            jnp.stack(places + [x, core]).astype(jnp.int32),
-            tuple(plan),
-            arrays,
-            tok,
-            tok_pair,
-            cot,
-            cot_part,
-            cot_rest,
-            kv,
-            start,
-            depth,
-            last,
-        )
-        own_sum, pair = results[:2]
+        places = jnp.stack(places + [x, core]).astype(jnp.int32)
+        rows_of = (tok, tok_pair, cot, cot_part, cot_rest)
+
+        def product(modes, kv):
+            return chunk_product(
+                places, tuple(plan), arrays, *rows_of, kv, start, depth, last, modes
+            )
+
+        if last:
+            own_sum, pair = product(("ig",), None)
+            results = product(("kv",), kv)
+        else:
+            own_sum, pair, kv = product(("kv", "ig"), kv)
         own_pieces.append(own_sum)
-        kv = results[2]
         got_pieces.append(x_send(pair))
-    keep, other_columns = results[2:]
+    keep, other_columns = results
     core_got = core_send(other_columns)
     pair_sum = pl.pallas_call(
         kv_pair_kernel,

time: 222 us -> 222 us (level)
  waiting for transfers between devices: 94.6 us -> 89.3 us
  Pallas kernels: 38 us -> 42.9 us
  local copies, waits for them, and re-layouts: 32.9 us -> 36.6 us
    all_to_all x1, waiting for transfers between devices: 6.19 us -> 0.01 us  [exchange(): lax.all_to_all(value, 'fsdp', split_axis=0, concat_axis=0, tiled=True)]
    pallas_call x2 -> x3, Pallas kernels: 16.9 us -> 20.9 us  [chunk_product(): pl.pallas_call(functools.partial(chunk_kernel, plan, len(arrays), modes,...]
    unnamed x86 -> x112, local copies, waits for them, and re-layouts: 32.5 us -> 36.2 us
  transfers between devices with their start and end apart: 26 -> 26, of which waited for: 15 -> 15; matrix products, arithmetic and copies ran while one was open for 0% -> 0% of each run, Pallas kernels for 12% -> 15%
where the time goes in v2:
time: 222 us; the launch traced here: 221 us
  waiting for transfers between devices  89.3 us (40%)
  Pallas kernels  42.9 us (19%)
  local copies, waits for them, and re-layouts  36.6 us (16%)
  starting transfers between devices  32.3 us (15%)
  blocking collectives  18.5 us (8%)
    ppermute x25, waiting for transfers between devices, send(): return lax.ppermute(value, axis, [(i, route(i)) for i in range(count)])  89.3 us
    unnamed x112, local copies, waits for them, and re-layouts  36.2 us
    ppermute x25, starting transfers between devices, send(): return lax.ppermute(value, axis, [(i, route(i)) for i in range(count)])  28.5 us
    pallas_call x3, Pallas kernels, chunk_product(): pl.pallas_call(functools.partial(chunk_kernel, plan, len(arrays), modes,...  20.9 us
    all_to_all x1, blocking collectives, exchange(): lax.all_to_all(value, 'fsdp', split_axis=0, concat_axis=0, tiled=True)  18.5 us
    pallas_call x1, Pallas kernels, paired(): pl.pallas_call(functools.partial(spread_kernel, blocks), name='spread', g...  7.8 us
  transfers between devices with their start and end apart: 26, of which 15 were waited for; matrix products, arithmetic and copies ran while one was open for 0% of the time, Pallas kernels for 15%

profile of v2, /device:TPU:0, one launch (start us, length us, event | category | flops | bytes accessed | tf_op | source)
XLA Modules:
  0.0 220.7 jit_solution(7981710587908572907)
XLA Ops:
  0.7 1.2 copy-done.10
  2.5 3.0 %collective-permute-start.12 = (bf16[1024,128]{1,0:T(8,128)(2,1)S(1)}, bf16[1024,128]{1,0:T(8,128)(2,1)S(1)}, u32[]{:S(2)}, u32[]{:S(2)}) collective-permute-start(bf16[1024,128]{1,0:T(8,128)(2,1)S(1)} %first.1), channel_id=1, source_target_pairs={{0,2},{2,0},{4,6},{6,4},{8,10},{10,8},{12,14},{14,12},{16,18},{18,... | collective-permute-start | bytes 786440 | tf_op jit(solution)/shard_map/ppermute | solution.py:39
  5.6 1.6 copy-done
  7.2 1.2 copy-done.2
  9.2 2.7 %collective-permute-done.12.theirs = bf16[1024,128]{1,0:T(8,128)(2,1)S(1)} collective-permute-done((bf16[1024,128]{1,0:T(8,128)(2,1)S(1)}, bf16[1024,128]{1,0:T(8,128)(2,1)S(1)}, u32[]{:S(2)}, u32[]{:S(2)}) %collective-permute-start.12) | collective-permute-done | bytes 262176 | tf_op jit(solution)/shard_map/ppermute | solution.py:39
  12.5 1.9 collective-permute-start.14
  14.4 1.5 collective-permute-start
  15.9 5.4 %collective-permute-done.theirs = bf16[1024,128]{1,0:T(8,128)(2,1)S(1)} collective-permute-done((bf16[1024,128]{1,0:T(8,128)(2,1)S(1)}, bf16[1024,128]{1,0:T(8,128)(2,1)S(1)}, u32[]{:S(2)}, u32[]{:S(2)}) %collective-permute-start) | collective-permute-done | bytes 262176 | tf_op jit(solution)/shard_map/ppermute | solution.py:39
  22.0 1.6 collective-permute-start.3
  24.4 1.5 collective-permute-start.9
  25.9 3.3 %collective-permute-done.14.refs_4_ = bf16[1024,256]{1,0:T(8,128)(2,1)S(1)} collective-permute-done((bf16[1024,256]{1,0:T(8,128)(2,1)S(1)}, bf16[1024,256]{1,0:T(8,128)(2,1)S(1)}, u32[]{:S(2)}, u32[]{:S(2)}) %collective-permute-start.14) | collective-permute-done | bytes 524320 | tf_op jit(solution)/shard_map/ppermute | solution.py:39
  29.2 1.7 collective-permute-start.1
  30.9 1.5 collective-permute-start.10
  32.4 8.1 %collective-permute-done.3.refs_4_ = bf16[1024,256]{1,0:T(8,128)(2,1)} collective-permute-done((bf16[1024,256]{1,0:T(8,128)(2,1)S(1)}, bf16[1024,256]{1,0:T(8,128)(2,1)}, u32[]{:S(2)}, u32[]{:S(2)}) %collective-permute-start.3) | collective-permute-done | bytes 524320 | tf_op jit(solution)/shard_map/ppermute | solution.py:39
  40.5 11.2 %collective-permute-done.16.refs_6_ = bf16[1024,256]{1,0:T(8,128)(2,1)} collective-permute-done((bf16[1024,256]{1,0:T(8,128)(2,1)S(1)}, bf16[1024,256]{1,0:T(8,128)(2,1)}, u32[]{:S(2)}, u32[]{:S(2)}) %collective-permute-start.16) | collective-permute-done | bytes 524320 | tf_op jit(solution)/shard_map/ppermute | solution.py:39
  52.6 1.7 collective-permute-start.13
  54.3 3.9 %collective-permute-done.10.refs_13_ = bf16[256,1024]{1,0:T(8,128)(2,1)S(1)} collective-permute-done((bf16[256,1024]{1,0:T(8,128)(2,1)S(1)}, bf16[256,1024]{1,0:T(8,128)(2,1)S(1)}, u32[]{:S(2)}, u32[]{:S(2)}) %collective-permute-start.10) | collective-permute-done | bytes 524320 | tf_op jit(solution)/shard_map/ppermute | solution.py:39
  59.8 1.7 collective-permute-start.15
  64.6 1.1 collective-permute-start.17
  65.7 8.5 %collective-permute-done.18.refs_8_ = bf16[1024,256]{1,0:T(8,128)(2,1)} collective-permute-done((bf16[1024,256]{1,0:T(8,128)(2,1)}, bf16[1024,256]{1,0:T(8,128)(2,1)}, u32[]{:S(2)}, u32[]{:S(2)}) %collective-permute-start.18) | collective-permute-done | bytes 524320 | tf_op jit(solution)/shard_map/ppermute | solution.py:39
  74.2 1.7 collective-permute-start.19
  77.9 1.7 collective-permute-start.6
  79.6 4.2 %collective-permute-done.7.refs_8_ = bf16[1024,256]{1,0:T(8,128)(2,1)} collective-permute-done((bf16[1024,256]{1,0:T(8,128)(2,1)}, bf16[1024,256]{1,0:T(8,128)(2,1)}, u32[]{:S(2)}, u32[]{:S(2)}) %collective-permute-start.7) | collective-permute-done | bytes 524320 | tf_op jit(solution)/shard_map/ppermute | solution.py:39
  83.8 1.5 collective-permute-start.8
  85.9 1.7 collective-permute-start.2
  87.5 9.6 %collective-permute-done.19.refs_9_ = bf16[1024,256]{1,0:T(8,128)(2,1)} collective-permute-done((bf16[1024,256]{1,0:T(8,128)(2,1)}, bf16[1024,256]{1,0:T(8,128)(2,1)}, u32[]{:S(2)}, u32[]{:S(2)}) %collective-permute-start.19) | collective-permute-done | bytes 524320 | tf_op jit(solution)/shard_map/ppermute | solution.py:39
  97.1 1.2 copy-done.13
  105.6 7.9 %shard_map.95 = (f32[256,1024]{1,0:T(8,128)S(1)}, bf16[256,1024]{1,0:T(8,128)(2,1)S(1)}, f32[512,2048]{1,0:T(8,128)S(1)}) custom-call(s32[10]{0:T(128)S(1)} %stack.59.refs_0_, bf16[1024,256]{1,0:T(8,128)(2,1)S(1)} %copy-done.34, bf16[2048,128]{1,0:T(8,128)(2,1)S(1)} %copy-done.16, bf16[1024,128]{1,0:T(8,128)(2,1)S(1)} %copy-done.54, ...), custom_call_target="tpu_custom_call" | custom-call | flops 4294967296 | bytes 12582912 | tf_op jit(solution)/shard_map/pallas_call | solution.py:160
  114.5 21.4 %collective-permute-done.2.refs_3_ = bf16[1024,128]{1,0:T(8,128)(2,1)S(1)} collective-permute-done((bf16[1024,128]{1,0:T(8,128)(2,1)S(1)}, bf16[1024,128]{1,0:T(8,128)(2,1)S(1)}, u32[]{:S(2)}, u32[]{:S(2)}) %collective-permute-start.2) | collective-permute-done | bytes 262176 | tf_op jit(solution)/shard_map/ppermute | solution.py:39
  135.9 6.5 %shard_map.96 = (f32[512,1024]{1,0:T(8,128)S(1)}, bf16[512,1024]{1,0:T(8,128)(2,1)}) custom-call(s32[10]{0:T(128)S(1)} %stack.59.refs_0_, bf16[1024,256]{1,0:T(8,128)(2,1)S(1)} %copy-done.8, bf16[2048,128]{1,0:T(8,128)(2,1)S(1)} %copy-done.16, bf16[1024,128]{1,0:T(8,128)(2,1)S(1)} %collective-permute-done.2.refs_3_, ...), custom_call_target="tpu_custom_call" | custom-call | flops 2147483648 | bytes 12582912 | tf_op jit(solution)/shard_map/pallas_call | solution.py:160
  142.5 1.3 copy-done.4
  144.1 2.2 copy-done.11
  146.3 1.2 copy-done.32
  147.5 2.1 fetch.1
  149.7 18.5 %all_to_all.10.got = bf16[16,48,256]{2,1,0:T(8,128)(2,1)S(1)} all-to-all(bf16[16,48,256]{2,1,0:T(8,128)(2,1)S(1)} %fetch.1), channel_id=1, replica_groups=mesh['fsdp'=16,'tp'=2] {'fsdp'}, dimensions={0} | all-to-all | bytes 786432 | tf_op jit(solution)/shard_map/all_to_all | solution.py:435
  170.3 1.2 collective-permute-done.22.other
  174.0 3.8 %all-to-all-start.1 = ((bf16[16,48,256]{2,1,0:T(8,128)(2,1)}), bf16[16,48,256]{2,1,0:T(8,128)(2,1)S(1)}, u32[]{:S(2)}, u32[]{:S(2)}) async-start(bf16[16,48,256]{2,1,0:T(8,128)(2,1)} %copy-done.35), calls=%async_computation.1 | async-start | bytes 786432 | tf_op jit(solution)/shard_map/all_to_all | solution.py:435
  177.8 1.9 collective-permute-start.23
  180.8 1.2 copy-done.14
  186.7 6.4 %shard_map.97 = (f32[256,1024]{1,0:T(8,128)S(1)}, bf16[256,1024]{1,0:T(8,128)(2,1)}) custom-call(s32[10]{0:T(128)S(1)} %copy-done.47, bf16[1024,256]{1,0:T(8,128)(2,1)S(1)} %copy-done.9, bf16[2048,128]{1,0:T(8,128)(2,1)S(1)} %copy-done.17, bf16[1024,128]{1,0:T(8,128)(2,1)S(1)} %copy-done.29, bf16[1024,256]{1,0:T(8,128)(2,1)} %collective-permute-done.3.refs_4_, ...), custom_call_target="tpu_custom_call" | custom-call | flops 2147483648 | bytes 12582912 | tf_op jit(solution)/shard_map/pallas_call | solution.py:160
  193.6 1.7 kv_pair.1
  195.3 1.4 collective-permute-start.21
  196.7 7.8 %spread.1 = (f32[512,16,256]{2,1,0:T(8,128)}, f32[1024,512]{1,0:T(8,128)}) custom-call(s32[32]{0:T(128)S(1)} %copy-done.45, s32[32,1]{1,0:T(8,128)S(1)} %reshape.42.ids_column, bf16[16,48,256]{2,1,0:T(8,128)(2,1)S(1)} %all-to-all-done.1.got), custom_call_target="tpu_custom_call" | custom-call | bytes 10485760 | tf_op jit(solution)/shard_map/spread/pallas_call | solution.py:484
  204.5 1.2 copy-done.27
  205.7 1.8 shard_map.98.refs_4_
  208.3 2.3 %shard_map.99 = bf16[256,4096]{1,0:T(8,128)(2,1)} custom-call(s32[2]{0:T(128)S(1)} %copy-done.43, bf16[256,1024]{1,0:T(8,128)(2,1)} %collective-permute-done.23.refs_0_, bf16[256,1024]{1,0:T(8,128)(2,1)S(1)} %collective-permute-done.24.refs_1_, bf16[256,16]{1,0:T(8,128)(2,1)S(1)} %copy-done.37, ...), custom_call_target="tpu_custom_call", output_to_operand_aliasing={{}: (5, {})} | custom-call | flops 16777216 | bytes 4194304 | tf_op jit(solution)/shard_map/pallas_call | solution.py:332
  210.6 7.7 %collective-permute-done.21.pair_got = bf16[256,1024]{1,0:T(8,128)(2,1)S(1)} collective-permute-done((bf16[256,1024]{1,0:T(8,128)(2,1)S(1)}, bf16[256,1024]{1,0:T(8,128)(2,1)S(1)}, u32[]{:S(2)}, u32[]{:S(2)}) %collective-permute-start.21) | collective-permute-done | bytes 524320 | tf_op jit(solution)/shard_map/ppermute | solution.py:39
  218.3 2.4 %kv_end.1 = bf16[256,1024]{1,0:T(8,128)(2,1)} custom-call(f32[512,1024]{1,0:T(8,128)S(1)} %copy-done.6, bf16[512,1024]{1,0:T(8,128)(2,1)} %collective-permute-done.20.got.core_got, bf16[256,1024]{1,0:T(8,128)(2,1)S(1)} %collective-permute-done.21.pair_got, bf16[256,16]{1,0:T(8,128)(2,1)S(1)} %copy-done.41, bf16[2,16,1024]{2,1,0:T(8,128)(2,1)S(1)} %copy-done.39), custom_call_target="tpu_custom_call" | custom-call | flops 8388608 | bytes 3145728 | tf_op jit(solution)/shard_map/kv_end/pallas_call | solution.py:542
  (137 shorter events, 31.5 us)
Async XLA Ops:
  1.9 19.4 %copy-start.42 = (s32[2]{0:T(128)}, s32[2]{0:T(128)S(1)}, u32[]{:S(2)}) copy-start(s32[2]{0:T(128)S(1)} %pad_add_fusion.place) | copy-start | bytes 28
  2.5 9.3 %collective-permute-start.12 = (bf16[1024,128]{1,0:T(8,128)(2,1)S(1)}, bf16[1024,128]{1,0:T(8,128)(2,1)S(1)}, u32[]{:S(2)}, u32[]{:S(2)}) collective-permute-start(bf16[1024,128]{1,0:T(8,128)(2,1)S(1)} %first.1), channel_id=1, source_target_pairs={{0,2},{2,0},{4,6},{6,4},{8,10},{10,8},{12,14},{14,12},{16,18},{18,... | collective-permute-start | bytes 786440 | tf_op jit(solution)/shard_map/ppermute | solution.py:39
  5.6 1.6 copy-start
  8.4 88.7 %copy-start.3 = (bf16[2,128,2048]{2,1,0:T(8,128)(2,1)S(1)}, bf16[2,128,2048]{2,1,0:T(8,128)(2,1)}, u32[]{:S(2)}) copy-start(bf16[2,128,2048]{2,1,0:T(8,128)(2,1)} %param.8) | copy-start | bytes 3145732
  9.1 88.0 %copy-start.1 = (bf16[2,128,4096]{2,1,0:T(8,128)(2,1)S(1)}, bf16[2,128,4096]{2,1,0:T(8,128)(2,1)}, u32[]{:S(2)}) copy-start(bf16[2,128,4096]{2,1,0:T(8,128)(2,1)} %param.6) | copy-start | bytes 6291460
  12.5 63.5 %copy-start.33 = (bf16[1024,256]{1,0:T(8,128)(2,1)}, bf16[1024,256]{1,0:T(8,128)(2,1)S(1)}, u32[]{:S(2)}) copy-start(bf16[1024,256]{1,0:T(8,128)(2,1)S(1)} %shard_map.94.refs_1_) | copy-start | bytes 1572868
  12.5 16.7 %collective-permute-start.14 = (bf16[1024,256]{1,0:T(8,128)(2,1)S(1)}, bf16[1024,256]{1,0:T(8,128)(2,1)S(1)}, u32[]{:S(2)}, u32[]{:S(2)}) collective-permute-start(bf16[1024,256]{1,0:T(8,128)(2,1)S(1)} %shard_map.94.refs_1_), channel_id=1, source_target_pairs={{0,8},{2,10},{4,12},{6,14},{8,16},{10,18},{12,20},{14,22},{16,24},... | collective-permute-start | bytes 1572872 | tf_op jit(solution)/shard_map/ppermute | solution.py:39
  14.4 6.9 %collective-permute-start = (bf16[1024,128]{1,0:T(8,128)(2,1)S(1)}, bf16[1024,128]{1,0:T(8,128)(2,1)S(1)}, u32[]{:S(2)}, u32[]{:S(2)}) collective-permute-start(bf16[1024,128]{1,0:T(8,128)(2,1)S(1)} %get-tuple-element.24), channel_id=1, source_target_pairs={{0,2},{2,0},{4,6},{6,4},{8,10},{10,8},{12,14},{14,12},{16,18},{18,... | collective-permute-start | bytes 786440 | tf_op jit(solution)/shard_map/ppermute | solution.py:39
  22.0 18.6 %collective-permute-start.3 = (bf16[1024,256]{1,0:T(8,128)(2,1)S(1)}, bf16[1024,256]{1,0:T(8,128)(2,1)}, u32[]{:S(2)}, u32[]{:S(2)}) collective-permute-start(bf16[1024,256]{1,0:T(8,128)(2,1)S(1)} %shard_map.93.refs_1_), channel_id=1, source_target_pairs={{0,8},{2,10},{4,12},{6,14},{8,16},{10,18},{12,20},{14,22},{16,24},... | collective-permute-start | bytes 1572872 | tf_op jit(solution)/shard_map/ppermute | solution.py:39
  24.4 39.3 %collective-permute-start.9 = (bf16[256,2048]{1,0:T(8,128)(2,1)S(1)}, bf16[256,2048]{1,0:T(8,128)(2,1)S(1)}, u32[]{:S(2)}, u32[]{:S(2)}) collective-permute-start(bf16[256,2048]{1,0:T(8,128)(2,1)S(1)} %get-tuple-element.25), channel_id=1, source_target_pairs={{0,2},{2,0},{4,6},{6,4},{8,10},{10,8},{12,14},{14,12},{16,18},{18,... | collective-permute-start | bytes 3145736 | tf_op jit(solution)/shard_map/ppermute | solution.py:39
  29.2 22.6 %collective-permute-start.16 = (bf16[1024,256]{1,0:T(8,128)(2,1)S(1)}, bf16[1024,256]{1,0:T(8,128)(2,1)}, u32[]{:S(2)}, u32[]{:S(2)}) collective-permute-start(bf16[1024,256]{1,0:T(8,128)(2,1)S(1)} %collective-permute-done.14.refs_4_), channel_id=1, source_target_pairs={{0,8},{2,10},{4,12},{6,14},{8,16},{10,18},{12,20},{14,22},{16,24},... | collective-permute-start | bytes 1572872 | tf_op jit(solution)/shard_map/ppermute | solution.py:39
  29.2 22.6 %collective-permute-start.1 = (bf16[2048,128]{1,0:T(8,128)(2,1)S(1)}, bf16[2048,128]{1,0:T(8,128)(2,1)S(1)}, u32[]{:S(2)}, u32[]{:S(2)}) collective-permute-start(bf16[2048,128]{1,0:T(8,128)(2,1)S(1)} %get-tuple-element.23.mine), channel_id=1, source_target_pairs={{0,4},{2,6},{4,0},{6,2},{8,12},{10,14},{12,8},{14,10},{16,20},{18,... | collective-permute-start | bytes 1572872 | tf_op jit(solution)/shard_map/ppermute | solution.py:39
  30.9 27.3 %collective-permute-start.10 = (bf16[256,1024]{1,0:T(8,128)(2,1)S(1)}, bf16[256,1024]{1,0:T(8,128)(2,1)S(1)}, u32[]{:S(2)}, u32[]{:S(2)}) collective-permute-start(bf16[256,1024]{1,0:T(8,128)(2,1)S(1)} %get-tuple-element.26), channel_id=1, source_target_pairs={{0,2},{2,0},{4,6},{6,4},{8,10},{10,8},{12,14},{14,12},{16,18},{18,... | collective-permute-start | bytes 1572872 | tf_op jit(solution)/shard_map/ppermute | solution.py:39
  40.5 22.5 %collective-permute-start.5 = (bf16[1024,256]{1,0:T(8,128)(2,1)}, bf16[1024,256]{1,0:T(8,128)(2,1)}, u32[]{:S(2)}, u32[]{:S(2)}) collective-permute-start(bf16[1024,256]{1,0:T(8,128)(2,1)} %collective-permute-done.3.refs_4_), channel_id=1, source_target_pairs={{0,8},{2,10},{4,12},{6,14},{8,16},{10,18},{12,20},{14,22},{16,24},... | collective-permute-start | bytes 1572872 | tf_op jit(solution)/shard_map/ppermute | solution.py:39
  51.8 22.5 %collective-permute-start.18 = (bf16[1024,256]{1,0:T(8,128)(2,1)}, bf16[1024,256]{1,0:T(8,128)(2,1)}, u32[]{:S(2)}, u32[]{:S(2)}) collective-permute-start(bf16[1024,256]{1,0:T(8,128)(2,1)} %collective-permute-done.16.refs_6_), channel_id=1, source_target_pairs={{0,8},{2,10},{4,12},{6,14},{8,16},{10,18},{12,20},{14,22},{16,24},... | collective-permute-start | bytes 1572872 | tf_op jit(solution)/shard_map/ppermute | solution.py:39
  52.6 6.5 %collective-permute-start.13 = (bf16[1024,128]{1,0:T(8,128)(2,1)S(1)}, bf16[1024,128]{1,0:T(8,128)(2,1)S(1)}, u32[]{:S(2)}, u32[]{:S(2)}) collective-permute-start(bf16[1024,128]{1,0:T(8,128)(2,1)S(1)} %collective-permute-done.12.theirs), channel_id=1, source_target_pairs={{0,4},{2,6},{4,0},{6,2},{8,12},{10,14},{12,8},{14,10},{16,20},{18,... | collective-permute-start | bytes 786440 | tf_op jit(solution)/shard_map/ppermute | solution.py:39
  58.2 17.7 %collective-permute-start.11 = (bf16[256,1024]{1,0:T(8,128)(2,1)S(1)}, bf16[256,1024]{1,0:T(8,128)(2,1)S(1)}, u32[]{:S(2)}, u32[]{:S(2)}) collective-permute-start(bf16[256,1024]{1,0:T(8,128)(2,1)S(1)} %collective-permute-done.10.refs_13_), channel_id=1, source_target_pairs={{0,1},{1,0},{2,3},{3,2},{4,5},{5,4},{6,7},{7,6},{8,9},{9,8},{10,11... | collective-permute-start | bytes 1572872 | tf_op jit(solution)/shard_map/ppermute | solution.py:39
  59.8 17.3 %collective-permute-start.15 = (bf16[1024,256]{1,0:T(8,128)(2,1)S(1)}, bf16[1024,256]{1,0:T(8,128)(2,1)S(1)}, u32[]{:S(2)}, u32[]{:S(2)}) collective-permute-start(bf16[1024,256]{1,0:T(8,128)(2,1)S(1)} %collective-permute-done.14.refs_4_), channel_id=1, source_target_pairs={{0,4},{2,6},{4,0},{6,2},{8,12},{10,14},{12,8},{14,10},{16,20},{18,... | collective-permute-start | bytes 1572872 | tf_op jit(solution)/shard_map/ppermute | solution.py:39
  63.0 20.8 %collective-permute-start.7 = (bf16[1024,256]{1,0:T(8,128)(2,1)}, bf16[1024,256]{1,0:T(8,128)(2,1)}, u32[]{:S(2)}, u32[]{:S(2)}) collective-permute-start(bf16[1024,256]{1,0:T(8,128)(2,1)} %collective-permute-done.5.refs_6_), channel_id=1, source_target_pairs={{0,8},{2,10},{4,12},{6,14},{8,16},{10,18},{12,20},{14,22},{16,24},... | collective-permute-start | bytes 1572872 | tf_op jit(solution)/shard_map/ppermute | solution.py:39
  64.6 21.3 %collective-permute-start.17 = (bf16[1024,256]{1,0:T(8,128)(2,1)}, bf16[1024,256]{1,0:T(8,128)(2,1)}, u32[]{:S(2)}, u32[]{:S(2)}) collective-permute-start(bf16[1024,256]{1,0:T(8,128)(2,1)} %collective-permute-done.16.refs_6_), channel_id=1, source_target_pairs={{0,4},{2,6},{4,0},{6,2},{8,12},{10,14},{12,8},{14,10},{16,20},{18,... | collective-permute-start | bytes 1572872 | tf_op jit(solution)/shard_map/ppermute | solution.py:39
  74.2 22.9 %collective-permute-start.19 = (bf16[1024,256]{1,0:T(8,128)(2,1)}, bf16[1024,256]{1,0:T(8,128)(2,1)}, u32[]{:S(2)}, u32[]{:S(2)}) collective-permute-start(bf16[1024,256]{1,0:T(8,128)(2,1)} %collective-permute-done.18.refs_8_), channel_id=1, source_target_pairs={{0,4},{2,6},{4,0},{6,2},{8,12},{10,14},{12,8},{14,10},{16,20},{18,... | collective-permute-start | bytes 1572872 | tf_op jit(solution)/shard_map/ppermute | solution.py:39
  76.8 59.1 %collective-permute-start.4 = (bf16[1024,256]{1,0:T(8,128)(2,1)}, bf16[1024,256]{1,0:T(8,128)(2,1)}, u32[]{:S(2)}, u32[]{:S(2)}) collective-permute-start(bf16[1024,256]{1,0:T(8,128)(2,1)} %collective-permute-done.3.refs_4_), channel_id=1, source_target_pairs={{0,4},{2,6},{4,0},{6,2},{8,12},{10,14},{12,8},{14,10},{16,20},{18,... | collective-permute-start | bytes 1572872 | tf_op jit(solution)/shard_map/ppermute | solution.py:39
  77.9 58.0 %collective-permute-start.6 = (bf16[1024,256]{1,0:T(8,128)(2,1)}, bf16[1024,256]{1,0:T(8,128)(2,1)}, u32[]{:S(2)}, u32[]{:S(2)}) collective-permute-start(bf16[1024,256]{1,0:T(8,128)(2,1)} %collective-permute-done.5.refs_6_), channel_id=1, source_target_pairs={{0,4},{2,6},{4,0},{6,2},{8,12},{10,14},{12,8},{14,10},{16,20},{18,... | collective-permute-start | bytes 1572872 | tf_op jit(solution)/shard_map/ppermute | solution.py:39
  83.8 52.1 %collective-permute-start.8 = (bf16[1024,256]{1,0:T(8,128)(2,1)}, bf16[1024,256]{1,0:T(8,128)(2,1)}, u32[]{:S(2)}, u32[]{:S(2)}) collective-permute-start(bf16[1024,256]{1,0:T(8,128)(2,1)} %collective-permute-done.7.refs_8_), channel_id=1, source_target_pairs={{0,4},{2,6},{4,0},{6,2},{8,12},{10,14},{12,8},{14,10},{16,20},{18,... | collective-permute-start | bytes 1572872 | tf_op jit(solution)/shard_map/ppermute | solution.py:39
  85.4 50.5 %copy-start.46 = (s32[10]{0:T(128)}, s32[10]{0:T(128)S(1)}, u32[]{:S(2)}) copy-start(s32[10]{0:T(128)S(1)} %stack.59.refs_0_) | copy-start | bytes 124
  85.4 50.5 %copy-start.8 = (bf16[1024,256]{1,0:T(8,128)(2,1)S(1)}, bf16[1024,256]{1,0:T(8,128)(2,1)}, u32[]{:S(2)}) copy-start(bf16[1024,256]{1,0:T(8,128)(2,1)} %copy-done.7) | copy-start | bytes 1572868
  85.9 50.0 %collective-permute-start.2 = (bf16[1024,128]{1,0:T(8,128)(2,1)S(1)}, bf16[1024,128]{1,0:T(8,128)(2,1)S(1)}, u32[]{:S(2)}, u32[]{:S(2)}) collective-permute-start(bf16[1024,128]{1,0:T(8,128)(2,1)S(1)} %collective-permute-done.theirs), channel_id=1, source_target_pairs={{0,4},{2,6},{4,0},{6,2},{8,12},{10,14},{12,8},{14,10},{16,20},{18,... | collective-permute-start | bytes 786440 | tf_op jit(solution)/shard_map/ppermute | solution.py:39
  114.5 21.4 %copy-start.52 = (bf16[256,1024]{1,0:T(8,128)(2,1)}, bf16[256,1024]{1,0:T(8,128)(2,1)S(1)}, u32[]{:S(2)}) copy-start(bf16[256,1024]{1,0:T(8,128)(2,1)S(1)} %get-tuple-element.33) | copy-start | bytes 1572868
  135.9 6.6 %copy-start.28 = (bf16[1024,128]{1,0:T(8,128)(2,1)}, bf16[1024,128]{1,0:T(8,128)(2,1)S(1)}, u32[]{:S(2)}) copy-start(bf16[1024,128]{1,0:T(8,128)(2,1)S(1)} %collective-permute-done.2.refs_3_) | copy-start | bytes 786436
  135.9 7.9 %copy-start.55 = (s32[2,16]{1,0:T(2,128)S(1)}, s32[2,16]{1,0:T(2,128)}, u32[]{:S(2)}) copy-start(s32[2,16]{1,0:T(2,128)} %param.9) | copy-start | bytes 388
  143.8 49.8 %collective-permute-start.20 = (bf16[512,1024]{1,0:T(8,128)(2,1)}, bf16[512,1024]{1,0:T(8,128)(2,1)}, u32[]{:S(2)}, u32[]{:S(2)}) collective-permute-start(bf16[512,1024]{1,0:T(8,128)(2,1)} %get-tuple-element.29), channel_id=1, source_target_pairs={{0,1},{1,0},{2,3},{3,2},{4,5},{5,4},{6,7},{7,6},{8,9},{9,8},{10,11... | collective-permute-start | bytes 3145736 | tf_op jit(solution)/shard_map/ppermute | solution.py:39
  144.1 5.6 %copy-start.44 = (s32[32]{0:T(128)}, s32[32]{0:T(128)S(1)}, u32[]{:S(2)}) copy-start(s32[32]{0:T(128)S(1)} %reshape_reshape.3.ids) | copy-start | bytes 388
  144.1 2.2 copy-start.11
  170.3 1.2 collective-permute-start.22
  174.0 22.6 %all-to-all-start.1 = ((bf16[16,48,256]{2,1,0:T(8,128)(2,1)}), bf16[16,48,256]{2,1,0:T(8,128)(2,1)S(1)}, u32[]{:S(2)}, u32[]{:S(2)}) async-start(bf16[16,48,256]{2,1,0:T(8,128)(2,1)} %copy-done.35), calls=%async_computation.1 | async-start | bytes 786432 | tf_op jit(solution)/shard_map/all_to_all | solution.py:435
  177.8 15.8 %copy-start.5 = (f32[512,1024]{1,0:T(8,128)S(1)}, f32[512,1024]{1,0:T(8,128)}, u32[]{:S(2)}) copy-start(f32[512,1024]{1,0:T(8,128)} %copy-done.4) | copy-start | bytes 6291460
  177.8 29.8 %collective-permute-start.23 = (bf16[256,1024]{1,0:T(8,128)(2,1)}, bf16[256,1024]{1,0:T(8,128)(2,1)}, u32[]{:S(2)}, u32[]{:S(2)}) collective-permute-start(bf16[256,1024]{1,0:T(8,128)(2,1)} %copy-done.52), channel_id=1, source_target_pairs={{0,2},{2,0},{4,6},{6,4},{8,10},{10,8},{12,14},{14,12},{16,18},{18,... | collective-permute-start | bytes 1572872 | tf_op jit(solution)/shard_map/ppermute | solution.py:39
  193.1 2.1 copy-start.26
  193.1 3.5 %copy-start.45 = (s32[32]{0:T(128)S(1)}, s32[32]{0:T(128)}, u32[]{:S(2)}) copy-start(s32[32]{0:T(128)} %copy-done.44) | copy-start | bytes 388
  193.1 11.3 %copy-start.25 = (f32[256,1024]{1,0:T(8,128)S(1)}, f32[256,1024]{1,0:T(8,128)}, u32[]{:S(2)}) copy-start(f32[256,1024]{1,0:T(8,128)} %copy-done.24) | copy-start | bytes 3145732
  193.2 11.3 %copy-start.31 = (bf16[2,16,4096]{2,1,0:T(8,128)(2,1)S(1)}, bf16[2,16,4096]{2,1,0:T(8,128)(2,1)}, u32[]{:S(2)}) copy-start(bf16[2,16,4096]{2,1,0:T(8,128)(2,1)} %copy-done.30) | copy-start | bytes 786436
  193.2 11.3 %copy-start.37 = (bf16[256,16]{1,0:T(8,128)(2,1)S(1)}, bf16[256,16]{1,0:T(8,128)(2,1)}, u32[]{:S(2)}) copy-start(bf16[256,16]{1,0:T(8,128)(2,1)} %copy-done.36) | copy-start | bytes 24580
  193.2 11.3 %copy-start.43 = (s32[2]{0:T(128)S(1)}, s32[2]{0:T(128)}, u32[]{:S(2)}) copy-start(s32[2]{0:T(128)} %copy-done.42) | copy-start | bytes 28
  193.2 15.1 %collective-permute-start.24 = (bf16[256,1024]{1,0:T(8,128)(2,1)}, bf16[256,1024]{1,0:T(8,128)(2,1)S(1)}, u32[]{:S(2)}, u32[]{:S(2)}) collective-permute-start(bf16[256,1024]{1,0:T(8,128)(2,1)} %get-tuple-element.34), channel_id=1, source_target_pairs={{0,2},{2,0},{4,6},{6,4},{8,10},{10,8},{12,14},{14,12},{16,18},{18,... | collective-permute-start | bytes 1572872 | tf_op jit(solution)/shard_map/ppermute | solution.py:39
  195.3 23.0 %collective-permute-start.21 = (bf16[256,1024]{1,0:T(8,128)(2,1)S(1)}, bf16[256,1024]{1,0:T(8,128)(2,1)S(1)}, u32[]{:S(2)}, u32[]{:S(2)}) collective-permute-start(bf16[256,1024]{1,0:T(8,128)(2,1)S(1)} %kv_pair.1), channel_id=1, source_target_pairs={{0,2},{2,0},{4,6},{6,4},{8,10},{10,8},{12,14},{14,12},{16,18},{18,... | collective-permute-start | bytes 1572872 | tf_op jit(solution)/shard_map/ppermute | solution.py:39
  207.5 10.7 %copy-start.6 = (f32[512,1024]{1,0:T(8,128)S(1)}, f32[512,1024]{1,0:T(8,128)}, u32[]{:S(2)}) copy-start(f32[512,1024]{1,0:T(8,128)} %copy-done.4) | copy-start | bytes 6291460
  207.5 10.7 %copy-start.39 = (bf16[2,16,1024]{2,1,0:T(8,128)(2,1)S(1)}, bf16[2,16,1024]{2,1,0:T(8,128)(2,1)}, u32[]{:S(2)}) copy-start(bf16[2,16,1024]{2,1,0:T(8,128)(2,1)} %copy-done.38) | copy-start | bytes 196612
  207.6 10.7 %copy-start.41 = (bf16[256,16]{1,0:T(8,128)(2,1)S(1)}, bf16[256,16]{1,0:T(8,128)(2,1)}, u32[]{:S(2)}) copy-start(bf16[256,16]{1,0:T(8,128)(2,1)} %copy-done.40) | copy-start | bytes 24580
  (34 other events, 32.4 us)
